TPU v7x, 128 devices: a whole 4x4x4 slice. The times are simulated.
128 devices in a mesh: gy: 16 (over y_hi, z, core), gz: 8 (over x, y_lo).
Axes of the slice: x: 4, y: 4 (y_hi: 2, y_lo: 2; y = y_hi * 2 + y_lo), z: 4, core: 2. Of those that a mesh axis runs over, the one named last changes fastest.
Arguments:
- field_in: bfloat16 [64, 256, 128, 256], P(None, 'gy', 'gz'), may hold values from -42 to 42
- spectral_weight: bfloat16 [32, 32, 32, 64, 128], P('gz', 'gy'), may hold values from -1.5258789e-05 to 1.5258789e-05
- point_weight: bfloat16 [64, 64], replicated, may hold values from -0.75 to 0.75
- point_bias: float32 [64], replicated, may hold values from -3 to 3
- out_weight: bfloat16 [64, 3], replicated, may hold values from -0.75 to 0.75
- out_bias: float32 [3], replicated, may hold values from -4 to 4
Outputs:
- loss_value: float32 [], replicated
- grad_spectral: float32 [32, 32, 32, 64, 128], P('gz', 'gy')
- grad_point: float32 [64, 64], replicated
- grad_point_bias: float32 [64], replicated
- grad_out: float32 [64, 3], replicated
- grad_out_bias: float32 [3], replicated
All inputs are finite; a program needn't handle non-finite values.
Results may differ from a plain program's by a relative error of at most 0.01.
Values may be sent and summed in bfloat16 or wider, within the bound.
A program may use at most 192 MiB of HBM per device.

v0:
```python
import math

import jax
import jax.numpy as jnp
from jax import lax
from jax.sharding import PartitionSpec as P

NX = 256
NY = 256
NZ = 128
MX = 32
MY = 32
MZ = 32


def with_halo(block, sides, width):
    for axis, dim in sides:
        count = lax.axis_size(axis)
        forward = [(i, i + 1) for i in range(count - 1)]
        backward = [(target, source) for source, target in forward]
        low = lax.ppermute(
            lax.slice_in_dim(block, block.shape[dim] - width, None, axis=dim), axis, forward
        )
        high = lax.ppermute(lax.slice_in_dim(block, 0, width, axis=dim), axis, backward)
        block = jnp.concatenate([low, block, high], axis=dim)
    return block


def frequencies(mode_count, mode_total):
    mode_index = jnp.arange(mode_count, dtype=jnp.int32)
    return jnp.where(mode_index < mode_total // 2, mode_index, mode_index - mode_total)


def twiddle(positions, wave_numbers, length):
    product = positions[:, None] * wave_numbers[None, :] % length
    phases = product.astype(jnp.float32) * (2.0 * math.pi / length)
    return (jnp.cos(phases).astype(jnp.bfloat16), jnp.sin(phases).astype(jnp.bfloat16))


def rotate(with_cos, with_sin, forward):
    half_width = with_cos.shape[-1] // 2
    cos_real, cos_imag = (with_cos[..., :half_width], with_cos[..., half_width:])
    sin_real, sin_imag = (with_sin[..., :half_width], with_sin[..., half_width:])
    if forward:
        return jnp.concatenate([cos_real + sin_imag, cos_imag - sin_real], axis=-1)
    return jnp.concatenate([cos_real - sin_imag, cos_imag + sin_real], axis=-1)


def x_tables(length, mode_total):
    cos_part, sin_part = twiddle(
        jnp.arange(length, dtype=jnp.int32), frequencies(mode_total, mode_total), length
    )
    forward_table = jnp.stack([cos_part, -sin_part], axis=1)
    inverse_table = jnp.stack([cos_part.T, -sin_part.T], axis=0)
    return (forward_table, inverse_table)


def cell_loss(field_b, slope_x, slope_y, slope_z):
    current_x = slope_y[2] - slope_z[1]
    current_y = slope_z[0] - slope_x[2]
    current_z = slope_x[1] - slope_y[0]
    force_x = current_y * field_b[2] - current_z * field_b[1]
    force_y = current_z * field_b[0] - current_x * field_b[2]
    force_z = current_x * field_b[1] - current_y * field_b[0]
    spread = slope_x[0] + slope_y[1] + slope_z[2]
    strength = field_b[0] * field_b[0] + field_b[1] * field_b[1] + field_b[2] * field_b[2] + 1.0
    return (force_x * force_x + force_y * force_y + force_z * force_z) / strength + spread * spread


def gelu_slope(pre_act):
    normal_cdf = 0.5 * (1.0 + lax.erf(pre_act * (1.0 / math.sqrt(2.0))))
    density = jnp.exp(-0.5 * pre_act * pre_act) * (1.0 / math.sqrt(2.0 * math.pi))
    return normal_cdf + pre_act * density


def to_modes(grid_field, factor, y_cells, z_cells, forward_table):
    channels, local_rows, local_depth = (
        grid_field.shape[0],
        grid_field.shape[1],
        grid_field.shape[2],
    )
    products = jnp.einsum(
        "cyzx,xpk->yzkpc", grid_field, forward_table, preferred_element_type=jnp.float32
    )
    x_modes = products.reshape(local_rows, local_depth, MX, 2 * channels).astype(jnp.bfloat16)
    y_cos, y_sin = twiddle(
        y_cells, frequencies(MY // lax.axis_size("gy") * lax.axis_size("gy"), MY), NY
    )
    with_cos = jnp.einsum("yzkc,yj->jzkc", x_modes, y_cos, preferred_element_type=jnp.float32)
    with_sin = jnp.einsum("yzkc,yj->jzkc", x_modes, y_sin, preferred_element_type=jnp.float32)
    y_modes = lax.psum_scatter(
        rotate(with_cos, with_sin, True), "gy", scatter_dimension=0, tiled=True
    ).astype(jnp.bfloat16)
    z_cos, z_sin = twiddle(
        z_cells, frequencies(MZ // lax.axis_size("gz") * lax.axis_size("gz"), MZ), NZ
    )
    with_cos = jnp.einsum("bzkc,zj->jbkc", y_modes, z_cos, preferred_element_type=jnp.float32)
    with_sin = jnp.einsum("bzkc,zj->jbkc", y_modes, z_sin, preferred_element_type=jnp.float32)
    summed = lax.psum_scatter(
        rotate(with_cos, with_sin, True), "gz", scatter_dimension=0, tiled=True
    )
    return (summed * factor).astype(jnp.bfloat16)


def from_modes(modes_out, y_cells, z_cells):
    portion = lax.all_gather(modes_out, "gz", axis=0, tiled=True)
    z_cos, z_sin = twiddle(z_cells, frequencies(portion.shape[0], MZ), NZ)
    with_cos = jnp.einsum("jbkc,zj->bzkc", portion, z_cos, preferred_element_type=jnp.float32)
    with_sin = jnp.einsum("jbkc,zj->bzkc", portion, z_sin, preferred_element_type=jnp.float32)
    z_back = rotate(with_cos, with_sin, False).astype(jnp.bfloat16)
    portion = lax.all_gather(z_back, "gy", axis=0, tiled=True)
    y_cos, y_sin = twiddle(y_cells, frequencies(portion.shape[0], MY), NY)
    with_cos = jnp.einsum("jzkc,yj->yzkc", portion, y_cos, preferred_element_type=jnp.float32)
    with_sin = jnp.einsum("jzkc,yj->yzkc", portion, y_sin, preferred_element_type=jnp.float32)
    return rotate(with_cos, with_sin, False).astype(jnp.bfloat16)


def mix_modes(modes_in, spectral_weight):
    channels = spectral_weight.shape[-2]
    with_real = jnp.einsum(
        "abki,abkio->abko",
        modes_in[..., :channels],
        spectral_weight,
        preferred_element_type=jnp.float32,
    )
    with_imag = jnp.einsum(
        "abki,abkio->abko",
        modes_in[..., channels:],
        spectral_weight,
        preferred_element_type=jnp.float32,
    )
    return jnp.concatenate(
        [
            with_real[..., :channels] - with_imag[..., channels:],
            with_real[..., channels:] + with_imag[..., :channels],
        ],
        axis=-1,
    ).astype(jnp.bfloat16)


def weight_grad(modes_in, grad_modes):
    channels = modes_in.shape[-1] // 2
    with_real = jnp.einsum(
        "abki,abko->abkio", modes_in[..., :channels], grad_modes, preferred_element_type=jnp.float32
    )
    with_imag = jnp.einsum(
        "abki,abko->abkio", modes_in[..., channels:], grad_modes, preferred_element_type=jnp.float32
    )
    return jnp.concatenate(
        [
            with_real[..., :channels] + with_imag[..., channels:],
            with_real[..., channels:] - with_imag[..., :channels],
        ],
        axis=-1,
    )


def on_device(field_in, spectral_weight, point_weight, point_bias, out_weight, out_bias):
    channels, local_rows, local_depth, x_count = field_in.shape
    y_cells = lax.axis_index("gy") * local_rows + jnp.arange(local_rows, dtype=jnp.int32)
    z_cells = lax.axis_index("gz") * local_depth + jnp.arange(local_depth, dtype=jnp.int32)
    forward_table, inverse_table = x_tables(x_count, MX)
    modes_in = to_modes(
        field_in, math.sqrt(MX * MY * MZ / (NX * NY * NZ)), y_cells, z_cells, forward_table
    )
    modes_out = mix_modes(modes_in, spectral_weight)
    y_back = from_modes(modes_out, y_cells, z_cells)
    spectral = jnp.einsum(
        "yzkpc,pkx->cyzx",
        y_back.reshape(local_rows, local_depth, MX, 2, channels),
        inverse_table,
        preferred_element_type=jnp.float32,
    )
    pointwise = jnp.einsum(
        "cyzx,co->oyzx", field_in, point_weight, preferred_element_type=jnp.float32
    )
    pre_act = spectral + pointwise + point_bias[:, None, None, None]
    hidden = jax.nn.gelu(pre_act, approximate=False).astype(jnp.bfloat16)
    b_field = (
        jnp.einsum("cyzx,cb->byzx", hidden, out_weight, preferred_element_type=jnp.float32)
        + out_bias[:, None, None, None]
    )
    padded = with_halo(b_field, (("gy", 1), ("gz", 2)), 2)
    widened = padded[:, 1:-1, 1:-1]
    x_padded = jnp.pad(widened, ((0, 0), (0, 0), (0, 0), (1, 1)))
    slope_x = (x_padded[..., 2:] - x_padded[..., :-2]) * 0.5
    slope_y = (padded[:, 2:, 1:-1] - padded[:, :-2, 1:-1]) * 0.5
    slope_z = (padded[:, 1:-1, 2:] - padded[:, 1:-1, :-2]) * 0.5
    cell_terms, pullback = jax.vjp(cell_loss, widened, slope_x, slope_y, slope_z)
    y_wide = lax.axis_index("gy") * local_rows - 1 + jnp.arange(local_rows + 2, dtype=jnp.int32)
    z_wide = lax.axis_index("gz") * local_depth - 1 + jnp.arange(local_depth + 2, dtype=jnp.int32)
    inside = ((y_wide >= 0) & (y_wide < NY))[:, None] & ((z_wide >= 0) & (z_wide < NZ))[None, :]
    weight_map = jnp.broadcast_to(
        jnp.where(inside, 1.0, 0.0)[:, :, None] / (NX * NY * NZ), cell_terms.shape
    ).astype(jnp.float32)
    grad_wide, grad_x, grad_y, grad_z = pullback(weight_map)
    gx_inner = jnp.pad(grad_x[:, 1:-1, 1:-1], ((0, 0), (0, 0), (0, 0), (1, 1)))
    grad_b = grad_wide[:, 1:-1, 1:-1] + (gx_inner[..., :-2] - gx_inner[..., 2:]) * 0.5
    grad_b = grad_b + (grad_y[:, :-2, 1:-1] - grad_y[:, 2:, 1:-1]) * 0.5
    grad_b = grad_b + (grad_z[:, 1:-1, :-2] - grad_z[:, 1:-1, 2:]) * 0.5
    loss_local = jnp.sum(cell_terms[1:-1, 1:-1])
    weights_f = out_weight.astype(jnp.float32)
    grad_hidden = jnp.zeros_like(pre_act)
    for component in range(3):
        grad_hidden = (
            grad_hidden + weights_f[:, component][:, None, None, None] * grad_b[component][None]
        )
    grad_pre = (grad_hidden * gelu_slope(pre_act)).astype(jnp.bfloat16)
    out_part = jnp.einsum(
        "cyzx,byzx->cb",
        hidden,
        grad_b,
        preferred_element_type=jnp.float32,
        precision=lax.Precision.HIGHEST,
    )
    out_bias_part = jnp.sum(grad_b, axis=(1, 2, 3))
    point_part = jnp.einsum("iyzx,oyzx->io", field_in, grad_pre, preferred_element_type=jnp.float32)
    point_bias_part = jnp.sum(grad_pre.astype(jnp.float32), axis=(1, 2, 3))
    totals = lax.psum(
        (loss_local, point_part, point_bias_part, out_part, out_bias_part), ("gy", "gz")
    )
    grad_modes = to_modes(grad_pre, 1.0, y_cells, z_cells, forward_table)
    grad_spectral = weight_grad(modes_in, grad_modes)
    return (totals[0] / (NX * NY * NZ), grad_spectral, totals[1], totals[2], totals[3], totals[4])


def solution(mesh):
    return jax.shard_map(
        on_device,
        mesh=mesh,
        in_specs=(P(None, "gy", "gz", None), P("gz", "gy", None, None, None), P(), P(), P(), P()),
        out_specs=(P(), P("gz", "gy", None, None, None), P(), P(), P(), P()),
        check_vma=False,
    )
```

profile of v0, /device:TPU:1, one launch (start us, length us, event | category | flops | bytes accessed | tf_op | source)
XLA Modules:
  0.0 781.1 jit_solution(12357975820388527888)
XLA Ops:
  7.7 13.6 %convert_bitcast_fusion.1 = bf16[16,16,32,2,64]{4,2,1,0,3:T(8,128)(2,1)S(1)} fusion(bf16[64,16,16,256]{3,2,1,0:T(8,128)(2,1)} %param.6, bf16[256,1,32]{0,2,1:T(8,128)(2,1)S(1)} %fusion.88, bf16[256,1,32]{0,2,1:T(8,128)(2,1)S(1)} %cosine_convert_fusion), kind=kOutput, calls=%fused_computation.58 | convolution fusion | flops 537985024 | bytes 10518528 | tf_op jit(solution)/shard_map/cyzx,xpk->yzkpc/dot_general | solution.py:82
  21.2 6.8 copy.89
  44.3 18.8 %slice_add_fusion.2 = (f32[32,16,32,64]{3,0,2,1:T(8,128)}, f32[32,16,32,64]{3,0,2,1:T(8,128)}) fusion(f32[32,16,32,128]{3,0,2,1:T(8,128)} %fusion.109, f32[32,16,32,128]{3,0,2,1:T(8,128)} %fusion.114), kind=kLoop, calls=%fused_computation.36 | loop fusion | flops 2097152 | bytes 25165824 | tf_op jit(solution)/shard_map/add | solution.py:45
  63.1 11.4 %pad_maximum_fusion = f32[32,16,32,128]{3,0,2,1:T(8,128)} fusion(f32[32,16,32,64]{3,0,2,1:T(8,128)} %get-tuple-element.63, f32[32,16,32,64]{3,0,2,1:T(8,128)} %get-tuple-element.62), kind=kLoop, calls=%fused_computation.37 | loop fusion | flops 2097152 | bytes 16777216 | tf_op jit(solution)/shard_map/concatenate | solution.py:45
  74.5 11.5 %copy.52 = f32[32,16,32,128]{3,2,1,0:T(8,128)} copy(f32[32,16,32,128]{3,0,2,1:T(8,128)} %pad_maximum_fusion) | data formatting | bytes 16777216 | tf_op jit(solution)/shard_map/concatenate | solution.py:45
  86.1 104.2 %reduce-scatter.5.cloned.1.call-done = f32[2,16,32,128]{3,2,1,0:T(8,128)} async-done(((f32[32,16,32,128]{3,2,1,0:T(8,128)}), f32[2,16,32,128]{3,2,1,0:T(8,128)}) %reduce-scatter.5.cloned.1.call-update) | async-done | bytes 524304 | tf_op jit(solution)/shard_map/reduce_scatter | solution.py:91
  194.9 34.7 %reduce-scatter.7.cloned.1.call-done = f32[4,2,32,128]{3,2,1,0:T(8,128)} async-done(((f32[32,2,32,128]{3,2,1,0:T(8,128)}), f32[4,2,32,128]{3,2,1,0:T(8,128)}) %reduce-scatter.7.cloned.1.call-update) | async-done | bytes 131088 | tf_op jit(solution)/shard_map/reduce_scatter | solution.py:99
  238.3 23.3 %all_gather.6 = bf16[32,2,32,128]{3,2,1,0:T(8,128)(2,1)S(1)} all-gather(bf16[4,2,32,128]{3,2,1,0:T(8,128)(2,1)S(1)} %pad_maximum_fusion.17), channel_id=1, replica_groups=mesh['gy'=16,'gz'=8] {'gz'}, dimensions={0}, use_global_device_ids=true | all-gather | bytes 589824 | tf_op jit(solution)/shard_map/all_gather | solution.py:106
  264.3 65.5 %all-gather.2.cloned.1.call-done = bf16[32,16,32,128]{3,2,1,0:T(8,128)(2,1)} async-done(((bf16[2,16,32,128]{3,2,1,0:T(8,128)(2,1)}), bf16[32,16,32,128]{3,2,1,0:T(8,128)(2,1)}) %all-gather.2.cloned.1.call-update) | async-done | bytes 4194320 | tf_op jit(solution)/shard_map/all_gather | solution.py:111
  340.8 8.1 %fusion.27 = f32[256,16,16,64,1]{0,3,4,2,1:T(8,128)} fusion(bf16[16,16,32,2,64]{4,0,2,1,3:T(8,128)(2,1)S(1)} %pad_maximum_fusion.3, bf16[1,32,256]{2,1,0:T(8,128)(2,1)S(1)} %fusion.87, bf16[1,32,256]{2,1,0:T(8,128)(2,1)S(1)} %cosine_convert_fusion.1), kind=kOutput, calls=%fused_computation.53 | convolution fusion | flops 536936448 | bytes 18907136 | tf_op jit(solution)/shard_map/yzkpc,pkx->cyzx/dot_general | solution.py:168
  348.9 19.3 %fusion.16 = (u16[64,16,256]{2,0,1:T(8,128)(2,1)S(1)}, f32[64,16,16,256]{3,0,2,1:T(8,128)}) fusion(f32[64]{0:T(128)S(1)} %copy-done.9, bf16[64,16,16,256]{3,2,1,0:T(8,128)(2,1)} %param.6, bf16[64,64]{1,0:T(8,128)(2,1)S(1)} %copy-done, f32[256,16,16,64,1]{0,3,4,2,1:T(8,128)} %fusion.27), kind=kOutput, calls=%fused_computation.30 | convolution fusion | flops 574357504 | bytes 42475776 | tf_op jit(solution)/shard_map/cyzx,co->oyzx/dot_general | solution.py:174
  368.2 39.0 %fusion.2 = bf16[64,16,16,256]{3,0,2,1:T(8,128)(2,1)S(1)} fusion(f32[64,16,16,256]{3,0,2,1:T(8,128)} %get-tuple-element.123, u16[64,16,256]{2,0,1:T(8,128)(2,1)S(1)} %get-tuple-element.122), kind=kLoop, calls=%fused_computation.4 | loop fusion | flops 285212672 | bytes 25690112 | tf_op jit(solution)/shard_map/convert_element_type | solution.py:178
  447.1 11.2 %convert_reduce_fusion = (f32[64]{0:T(128)S(1)}, bf16[64,16,16,256]{3,0,2,1:T(8,128)(2,1)S(1)}) fusion(f32[64,16,16,256]{3,0,2,1:T(8,128)S(1)} %bitcast.132, f32[16,16,256]{2,1,0:T(8,128)S(1)} %bitcast.135, f32[64]{0:T(128)S(1)} %get-tuple-element.120, f32[16,16,256]{2,1,0:T(8,128)S(1)} %bitcast.136, f32[64]{0:T(128)S(1)} %get-tuple-element.121, ...), kind=kLoop, calls=%fused_computation.15 | loop fusion | flops 71303104 | bytes 25953280 | tf_op jit(solution)/shard_map/reduce_sum | solution.py:218
  472.1 7.2 reshape.339
  488.6 18.5 %slice_add_fusion.1 = (f32[32,16,32,64]{3,0,2,1:T(8,128)}, f32[32,16,32,64]{3,0,2,1:T(8,128)}) fusion(f32[32,16,32,128]{3,0,2,1:T(8,128)} %fusion.106, f32[32,16,32,128]{3,0,2,1:T(8,128)} %fusion.111), kind=kLoop, calls=%fused_computation.34 | loop fusion | flops 2097152 | bytes 25165824 | tf_op jit(solution)/shard_map/add | solution.py:45
  507.1 11.2 %pad_maximum_fusion.1 = f32[32,16,32,128]{3,0,2,1:T(8,128)} fusion(f32[32,16,32,64]{3,0,2,1:T(8,128)} %get-tuple-element.61, f32[32,16,32,64]{3,0,2,1:T(8,128)} %get-tuple-element.60), kind=kLoop, calls=%fused_computation.38 | loop fusion | flops 2097152 | bytes 16777216 | tf_op jit(solution)/shard_map/concatenate | solution.py:45
  518.3 11.5 %copy.67 = f32[32,16,32,128]{3,2,1,0:T(8,128)} copy(f32[32,16,32,128]{3,0,2,1:T(8,128)} %pad_maximum_fusion.1) | data formatting | bytes 16777216 | tf_op jit(solution)/shard_map/concatenate | solution.py:45
  529.9 104.6 %reduce-scatter.9.cloned.1.call-done = f32[2,16,32,128]{3,2,1,0:T(8,128)} async-done(((f32[32,16,32,128]{3,2,1,0:T(8,128)}), f32[2,16,32,128]{3,2,1,0:T(8,128)}) %reduce-scatter.9.cloned.1.call-update) | async-done | bytes 524304 | tf_op jit(solution)/shard_map/reduce_scatter | solution.py:91
  639.8 9.0 %convolution_bitcast_fusion.2 = f32[64,3]{0,1:T(4,128)S(1)} fusion(bf16[64,16,16,256]{3,0,2,1:T(8,128)(2,1)} %copy-done.2, f32[3,16,16,256]{3,0,2,1:T(4,128)S(1)} %get-tuple-element.30), kind=kOutput, calls=%fused_computation.91 | convolution fusion | flops 150994944 | bytes 9175808 | tf_op jit(solution)/shard_map/cyzx,byzx->cb/dot_general | solution.py:209
  648.9 15.3 %fusion.45 = f32[64,64]{0,1:T(8,128)S(1)} fusion(bf16[64,16,16,256]{3,0,2,1:T(8,128)(2,1)} %copy-done.3, bf16[64,16,16,256]{3,2,1,0:T(8,128)(2,1)} %param.6), kind=kOutput, calls=%fused_computation.90 | convolution fusion | flops 536870912 | bytes 16793600 | tf_op jit(solution)/shard_map/iyzx,oyzx->io/dot_general | solution.py:217
  664.2 66.3 %all-reduce.20 = (f32[]{:T(128)}, f32[64,64]{0,1:T(8,128)S(1)}, f32[64]{0:T(128)}, f32[64,3]{0,1:T(4,128)}, f32[3]{0:T(128)}) all-reduce(f32[]{:T(128)} %slice_reduce_fusion, f32[64,64]{0,1:T(8,128)S(1)} %fusion.45, f32[64]{0:T(128)S(1)} %get-tuple-element.31, ...), channel_id=1, replica_groups=mesh['gy'=16,'gz'=8] {'gy','gz'}, use_global_device_ids=true, to_apply=%region_3.4 | all-reduce | flops 4356 | bytes 34848 | tf_op jit(solution)/shard_map/psum | solution.py:219
  732.8 8.4 %broadcast_multiply_fusion.1 = (f32[4,2,32,64,128]{4,3,2,1,0:T(8,128)}, f32[4,2,32,64,128]{4,3,2,1,0:T(8,128)}) fusion(f32[4,2,32,128]{3,2,1,0:T(8,128)S(1)} %convert_convert_fusion, f32[4,2,32,64]{3,2,1,0:T(8,128)S(1)} %copy-done.5, f32[4,2,32,64]{3,2,1,0:T(8,128)S(1)} %copy-done.6), kind=kLoop, calls=%fused_computation.56 | loop fusion | flops 4194304 | bytes 17039360 | tf_op jit(solution)/shard_map/abki,abko->abkio/dot_general | solution.py:143
  741.2 19.9 %slice_add_fusion = (f32[4,2,32,64,64]{4,3,2,1,0:T(8,128)}, f32[4,2,32,64,64]{4,3,2,1,0:T(8,128)}) fusion(f32[4,2,32,64,128]{4,3,2,1,0:T(8,128)} %get-tuple-element.114, f32[4,2,32,64,128]{4,3,2,1,0:T(8,128)} %get-tuple-element.113), kind=kLoop, calls=%fused_computation.32 | loop fusion | flops 2097152 | bytes 25165824 | tf_op jit(solution)/shard_map/add | solution.py:151
  761.1 12.1 %pad_maximum_fusion.2 = f32[4,2,32,64,128]{4,3,2,1,0:T(8,128)} fusion(f32[4,2,32,64,64]{4,3,2,1,0:T(8,128)} %get-tuple-element.59, f32[4,2,32,64,64]{4,3,2,1,0:T(8,128)} %get-tuple-element.58), kind=kLoop, calls=%fused_computation.39 | loop fusion | flops 2097152 | bytes 16777216 | tf_op jit(solution)/shard_map/concatenate | solution.py:149
  (116 shorter events, 113.2 us)
Async XLA Ops:
  7.2 341.8 %copy-start = (bf16[64,64]{1,0:T(8,128)(2,1)S(1)}, bf16[64,64]{1,0:T(8,128)(2,1)}, u32[]{:S(2)}) copy-start(bf16[64,64]{1,0:T(8,128)(2,1)} %param.8) | copy-start | bytes 24580
  7.2 183.1 %reduce-scatter.5.cloned.1.call-start = ((), (), s32[]{:S(2)}) async-start(), calls=%async_computation.4 | async-start | bytes 8912896 | tf_op jit(solution)/shard_map/reduce_scatter | solution.py:91
  86.0 143.6 %reduce-scatter.7.cloned.1.call-start = ((), (), s32[]{:S(2)}) async-start(), calls=%async_computation.5 | async-start | bytes 1179648 | tf_op jit(solution)/shard_map/reduce_scatter | solution.py:99
  194.9 135.0 %all-gather.2.cloned.1.call-start = ((), (), s32[]{:S(2)}) async-start(), calls=%async_computation.6 | async-start | bytes 4456448 | tf_op jit(solution)/shard_map/all_gather | solution.py:111
  263.8 370.7 %reduce-scatter.9.cloned.1.call-start = ((), (), s32[]{:S(2)}) async-start(), calls=%async_computation.7 | async-start | bytes 8912896 | tf_op jit(solution)/shard_map/reduce_scatter | solution.py:91
  329.8 4.9 copy-start.4
  340.8 8.1 %copy-start.9 = (f32[64]{0:T(128)S(1)}, f32[64]{0:T(128)}, u32[]{:S(2)}) copy-start(f32[64]{0:T(128)} %param.9) | copy-start | bytes 772
  368.2 39.1 %copy-start.7 = (bf16[64,3]{0,1:T(4,128)(2,1)S(1)}, bf16[64,3]{0,1:T(4,128)(2,1)}, u32[]{:S(2)}) copy-start(bf16[64,3]{0,1:T(4,128)(2,1)} %param.10) | copy-start | bytes 1156
  368.2 39.1 %copy-start.8 = (f32[3]{0:T(128)S(1)}, f32[3]{0:T(128)}, u32[]{:S(2)}) copy-start(f32[3]{0:T(128)} %param.11) | copy-start | bytes 40
  407.3 9.6 %copy-start.2 = (bf16[64,16,16,256]{3,0,2,1:T(8,128)(2,1)}, bf16[64,16,16,256]{3,0,2,1:T(8,128)(2,1)S(1)}, u32[]{:S(2)}) copy-start(bf16[64,16,16,256]{3,0,2,1:T(8,128)(2,1)S(1)} %fusion.2) | copy-start | bytes 25165828
  408.6 4.4 collective-permute-start
  410.5 6.3 collective-permute-start.1
  416.9 4.5 collective-permute-start.3
  419.1 6.7 collective-permute-start.2
  435.1 12.0 %slice-start = ((s8[16777216]{0:T(1024)(128)(4,1)}), s8[4194304]{0:T(1024)(128)(4,1)S(1)}, s32[]{:S(2)}) async-start(s8[16777216]{0:T(1024)(128)(4,1)} %bitcast.131), calls=%async_computation.9 | async-start | bytes 8388608
  436.2 10.8 %slice-start.1 = ((s8[16777216]{0:T(1024)(128)(4,1)}), s8[4194304]{0:T(1024)(128)(4,1)S(1)}, s32[]{:S(2)}) async-start(s8[16777216]{0:T(1024)(128)(4,1)} %bitcast.131), calls=%async_computation.10 | async-start | bytes 8388608
  440.7 6.4 slice-start.2
  442.2 4.8 slice-start.3
  458.3 3.4 copy-start.3
  529.9 202.0 %reduce-scatter.11.cloned.1.call-start = ((), (), s32[]{:S(2)}) async-start(), calls=%async_computation.8 | async-start | bytes 1179648 | tf_op jit(solution)/shard_map/reduce_scatter | solution.py:99
  648.8 83.9 %copy-start.5 = (f32[4,2,32,64]{3,2,1,0:T(8,128)S(1)}, f32[4,2,32,64]{3,2,1,0:T(8,128)}, u32[]{:S(2)}) copy-start(f32[4,2,32,64]{3,2,1,0:T(8,128)} %get-tuple-element.115) | copy-start | bytes 196612
  648.9 83.9 %copy-start.6 = (f32[4,2,32,64]{3,2,1,0:T(8,128)S(1)}, f32[4,2,32,64]{3,2,1,0:T(8,128)}, u32[]{:S(2)}) copy-start(f32[4,2,32,64]{3,2,1,0:T(8,128)} %get-tuple-element.116) | copy-start | bytes 196612
  761.1 12.1 %copy-start.1 = (bf16[64,64]{1,0:T(8,128)(2,1)S(1)}, bf16[64,64]{1,0:T(8,128)(2,1)}, u32[]{:S(2)}) copy-start(bf16[64,64]{1,0:T(8,128)(2,1)} %param.8) | copy-start | bytes 24580
Sparse Core Ops, SparseCore 0:
  86.1 104.1 reduce-scatter.4
  195.0 34.5 reduce-scatter.6
  263.9 65.8 all-gather.1
  530.0 104.5 reduce-scatter.8
  639.2 34.5 reduce-scatter.10
where the time goes:
time: 790 us; the launch traced here: 781 us
  waiting for transfers between devices  318 us (40%)
  other arithmetic  183 us (23%)
  matrix products  106 us (13%)
  blocking collectives  89.6 us (11%)
  local copies, waits for them, and re-layouts  59.1 us (7%)
  between operations  16.3 us (2%)
  starting transfers between devices  8.05 us (1%)
    reduce_scatter x2, waiting for transfers between devices, to_modes(): lax.psum_scatter(rotate(with_cos, with_sin, True), 'gy', scatter_dimensio...  209 us
    psum x1, blocking collectives, on_device(): lax.psum((loss_local, point_part, point_bias_part, out_part, out_bias_par...  66.3 us
    all_gather x1, waiting for transfers between devices, from_modes(): portion = lax.all_gather(z_back, 'gy', axis=0, tiled=True)  65.5 us
    convert_element_type x1, other arithmetic, on_device(): hidden = jax.nn.gelu(pre_act, approximate=False).astype(jnp.bfloat16)  39 us
    add x4, other arithmetic, rotate(): return jnp.concatenate([cos_real + sin_imag, cos_imag - sin_real], axis=-1)  38.6 us
    reduce_scatter x2, waiting for transfers between devices, to_modes(): lax.psum_scatter(rotate(with_cos, with_sin, True), 'gz', scatter_dimensio...  34.7 us
    convert_element_type x4, local copies, waits for them, and re-layouts, to_modes(): products.reshape(local_rows, local_depth, MX, 2 * channels)  27 us
    concatenate x4, local copies, waits for them, and re-layouts, rotate(): return jnp.concatenate([cos_real + sin_imag, cos_imag - sin_real], axis=-1)  26.2 us
  transfers between devices with their start and end apart: 9, of which 7 were waited for; matrix products, arithmetic and copies ran while one was open for 3% of the time, Pallas kernels for 0%

commit v1 on v0

v1 whole, which is shorter than its diff:
```python
import functools
import math

import jax
import jax.numpy as jnp
import numpy as np
from jax import lax
from jax.experimental import pallas as pl
from jax.experimental.pallas import tpu as pltpu
from jax.sharding import PartitionSpec as P

NX, NY, NZ = 256, 256, 128
M = 32
C = 64
GY, GZ = 16, 8
LY, LZ = 16, 16
QZ = 4
F32, BF16 = jnp.float32, jnp.bfloat16
SCALE = math.sqrt(M * M * M / (NX * NY * NZ))
CELLS = NX * NY * NZ
TAIL_SCALE = 0.24
TAIL = (0.08952144314768905, 0.15555677138787463, -0.15417797314110948, 0.6257953656595543, -0.6462531425989838, 0.5546601809863483, -0.12510264575439553)
MESH = pl.DeviceIdType.MESH
ANY = pl.BlockSpec(memory_space=pl.ANY)


def np_table(length):
    mode = np.arange(M)
    wave = np.where(mode < M // 2, mode, mode - M)
    product = (np.arange(length)[:, None] * wave[None, :]) % length
    phases = product.astype(np.float64) * (2.0 * math.pi / length)
    return np.cos(phases), np.sin(phases)


@functools.lru_cache(None)
def tables():
    cos_x, sin_x = np_table(NX)
    forward = np.zeros((40, NX))
    forward[:16] = cos_x[:, :16].T
    forward[16] = cos_x[:, 16]
    forward[17:32] = sin_x[:, 1:16].T
    forward[32] = sin_x[:, 16]
    inverse = np.zeros((40, NX))
    inverse[0:32:2] = forward[:16]
    inverse[1:32:2] = forward[16:32]
    inverse[32] = forward[32]
    cos_y, sin_y = np_table(NY)
    y_rows = np.kron(np.concatenate([cos_y, sin_y], axis=1).T, np.eye(QZ))
    cos_z, sin_z = np_table(NZ)
    z_rows = []
    for table in (cos_z, sin_z):
        cells = table.reshape(GZ, QZ, 4, M)
        for inner in range(4):
            part = cells[:, :, inner, :].reshape(GZ, QZ, GZ, 4)
            full = np.zeros((GZ, 2, 4, 2, GZ, 4, QZ))
            for gs in range(2):
                for ky2 in range(2):
                    full[:, gs, :, ky2, :, gs * 2 + ky2, :] = part.transpose(2, 3, 0, 1)
            z_rows.append(full.reshape(128, 128))
    z_rows = np.stack(z_rows).reshape(2, 4, 128, 128)
    return forward, inverse, y_rows, z_rows


def const(value):
    return jnp.asarray(value, BF16)


NT = (((1,), (1,)), ((), ()))
TN = (((0,), (0,)), ((), ()))


def dot(left, right, dims=(((1,), (0,)), ((), ()))):
    return lax.dot_general(left, right, dims, preferred_element_type=F32)


def whole(shape):
    return pl.BlockSpec(shape, lambda *_: (0,) * len(shape))


def params(limit=56 << 20):
    return pltpu.CompilerParams(vmem_limit_bytes=limit)


def swap_kernel(axis, count, modes, *refs):
    size = len(modes)
    srcs, dsts, sends, recvs = [refs[i * size : i * size + size] for i in range(4)]
    local = refs[4 * size]
    me = lax.axis_index(axis)
    barrier = pltpu.get_barrier_semaphore()
    for step in range(1, count):
        pl.semaphore_signal(
            barrier, inc=1, device_id={axis: (me + step) % count}, device_id_type=MESH
        )
    pl.semaphore_wait(barrier, count - 1)

    def remote(src, dst, send, recv, peer):
        return pltpu.make_async_remote_copy(
            src_ref=src, dst_ref=dst, send_sem=send, recv_sem=recv,
            device_id={axis: peer}, device_id_type=MESH,
        )

    copies, late = [], []
    for index, mode in enumerate(modes):
        src, dst, send, recv = srcs[index], dsts[index], sends[index], recvs[index]
        if mode == "to0":

            @pl.when(me != 0)
            def _(src=src, dst=dst, send=send, recv=recv):
                remote(src, dst.at[me], send.at[0], recv.at[me], 0).start()

            @pl.when(me == 0)
            def _(src=src, dst=dst, index=index):
                pltpu.make_async_copy(src, dst.at[0], local.at[index]).start()

            def finish(src=src, dst=dst, send=send, recv=recv, index=index):
                @pl.when(me != 0)
                def _():
                    remote(src, dst.at[me], send.at[0], recv.at[me], 0).wait_send()

                @pl.when(me == 0)
                def _():
                    pltpu.make_async_copy(src, dst.at[0], local.at[index]).wait()
                    for k in range(1, count):
                        remote(src, dst.at[k], send.at[0], recv.at[k], k).wait_recv()

            late.append(finish)
        elif mode == "from0":

            @pl.when(me == 0)
            def _(src=src, dst=dst, send=send, recv=recv, index=index):
                pltpu.make_async_copy(src.at[0], dst, local.at[index]).start()
                for k in range(1, count):
                    remote(src.at[k], dst, send.at[k], recv.at[0], k).start()

            def finish(src=src, dst=dst, send=send, recv=recv, index=index):
                @pl.when(me == 0)
                def _():
                    pltpu.make_async_copy(src.at[0], dst, local.at[index]).wait()
                    for k in range(1, count):
                        remote(src.at[k], dst, send.at[k], recv.at[0], k).wait_send()

                @pl.when(me != 0)
                def _():
                    remote(src.at[0], dst, send.at[0], recv.at[0], 0).wait_recv()

            late.append(finish)
        else:
            piece = (lambda p, src=src: src.at[p]) if mode == "swap" else (lambda p, src=src: src)
            copies.append(pltpu.make_async_copy(piece(me), dst.at[me], local.at[index]))
            for step in range(1, count):
                peer = (me + step) % count
                copies.append(
                    remote(piece(peer), dst.at[me], send.at[step], recv.at[step], peer)
                )
    for copy in copies:
        copy.start()
    for copy in copies:
        copy.wait()
    for finish in late:
        finish()


def swap(axis, count, collective_id, *operands):
    modes = tuple(mode for mode, _ in operands)
    args = [value for _, value in operands]
    outs = []
    for mode, value in operands:
        shape = value.shape
        if mode in ("all", "to0"):
            shape = (count,) + shape
        elif mode == "from0":
            shape = shape[1:]
        outs.append(jax.ShapeDtypeStruct(shape, value.dtype))
    size = len(args)
    result = pl.pallas_call(
        functools.partial(swap_kernel, axis, count, modes),
        out_shape=outs,
        in_specs=[ANY] * size,
        out_specs=[ANY] * size,
        scratch_shapes=[pltpu.SemaphoreType.DMA((count,))] * (2 * size)
        + [pltpu.SemaphoreType.DMA((size,))],
        compiler_params=pltpu.CompilerParams(
            collective_id=collective_id, has_side_effects=True
        ),
        name=f"swap_{collective_id}",
    )(*args)
    return result if size > 1 else result[0]


def deal_kernel(inward, src, dst, send, recv, local):
    g, h = lax.axis_index("gy"), lax.axis_index("gz")
    owners = [(2 * h + j % 2, j // 2) for j in range(GY)]
    holders = [(k, g // 2) for k in range(GY)]
    targets, sources = (holders, owners) if inward else (owners, holders)
    slot = h * 2 + g % 2 if inward else g

    def is_me(device):
        return jnp.logical_and(device[0] == g, device[1] == h)

    barrier = pltpu.get_barrier_semaphore()
    for device in sources:

        @pl.when(jnp.logical_not(is_me(device)))
        def _(device=device):
            pl.semaphore_signal(
                barrier, inc=1, device_id={"gy": device[0], "gz": device[1]}, device_id_type=MESH
            )

    diagonal = g // 2 == h
    pl.semaphore_wait(barrier, jnp.where(diagonal, GY - 1, GY))

    def outgoing(j):
        return pltpu.make_async_remote_copy(
            src_ref=src.at[j],
            dst_ref=dst.at[slot],
            send_sem=send.at[j],
            recv_sem=recv.at[slot],
            device_id={"gy": targets[j][0], "gz": targets[j][1]},
            device_id_type=MESH,
        )

    def incoming(j):
        return pltpu.make_async_remote_copy(
            src_ref=src.at[j],
            dst_ref=dst.at[j],
            send_sem=send.at[j],
            recv_sem=recv.at[j],
            device_id={"gy": sources[j][0], "gz": sources[j][1]},
            device_id_type=MESH,
        )

    for j in range(GY):
        mine = is_me(targets[j])

        @pl.when(jnp.logical_not(mine))
        def _(j=j):
            outgoing(j).start()

        @pl.when(mine)
        def _(j=j):
            copy = pltpu.make_async_copy(src.at[j], dst.at[slot], local.at[0])
            copy.start()
            copy.wait()

    for j in range(GY):

        @pl.when(jnp.logical_not(is_me(targets[j])))
        def _(j=j):
            outgoing(j).wait_send()

        @pl.when(jnp.logical_not(is_me(sources[j])))
        def _(j=j):
            incoming(j).wait_recv()


def deal(inward, collective_id, src):
    return pl.pallas_call(
        functools.partial(deal_kernel, inward),
        out_shape=jax.ShapeDtypeStruct(src.shape, src.dtype),
        in_specs=[ANY],
        out_specs=ANY,
        scratch_shapes=[pltpu.SemaphoreType.DMA((GY,))] * 2 + [pltpu.SemaphoreType.DMA((1,))],
        compiler_params=pltpu.CompilerParams(
            collective_id=collective_id, has_side_effects=True
        ),
        name=f"deal_{collective_id}",
    )(src)


def emit_rows(rows_ref, out_ref, extra_ref):
    for half in range(2):
        lanes = slice(half * 128, half * 128 + 128)
        for g in range(GY):
            for part in range(2):
                start = (part * GY + g) * 64
                out_ref[g, part, :, lanes] = rows_ref[half, start : start + 64, :].astype(BF16)
        extra_ref[:, lanes] = rows_ref[half, 2048:2112, :].astype(BF16)


def put_rows(rows_ref, start, value):
    for half in range(2):
        rows_ref[half, pl.ds(start, 40, stride=64), :] = value[:, half * 128 : half * 128 + 128]


def x_kernel(field_ref, table_ref, cells_ref, out_ref, extra_ref, stage, rows):
    y = pl.program_id(0)
    for half in range(2):
        lanes = slice(half * 128, half * 128 + 128)
        stage[half] = field_ref[:, 0, :, lanes].astype(F32).reshape(C * LZ, 128)
        for z in range(LZ):
            cells_ref[0, z, :, lanes] = stage[half, pl.ds(z, C, stride=LZ), :].astype(BF16)
    for q in range(QZ):
        block = cells_ref[0, q * 4 : q * 4 + 4].reshape(4 * C, NX)
        put_rows(rows, y * QZ + q, dot(table_ref[...], block, NT))

    @pl.when(y == LY - 1)
    def _():
        emit_rows(rows, out_ref, extra_ref)


def x_transform(field_in):
    forward = const(tables()[0])
    return pl.pallas_call(
        x_kernel,
        grid=(LY,),
        in_specs=[
            pl.BlockSpec((C, 1, LZ, NX), lambda y: (0, y, 0, 0)),
            whole((40, NX)),
        ],
        out_specs=[
            pl.BlockSpec((1, LZ, C, NX), lambda y: (y, 0, 0, 0)),
            whole((GY, 2, 64, NX)),
            whole((64, NX)),
        ],
        out_shape=[
            jax.ShapeDtypeStruct((LY, LZ, C, NX), BF16),
            jax.ShapeDtypeStruct((GY, 2, 64, NX), BF16),
            jax.ShapeDtypeStruct((64, NX), BF16),
        ],
        scratch_shapes=[pltpu.VMEM((2, C * LZ, 128), F32), pltpu.VMEM((2, 40 * 64, 128), F32)],
        compiler_params=params(),
        name="x_transform",
    )(field_in, forward)


def y_kernel(first_ref, src_ref, extra_ref, table_ref, out_ref):
    first = first_ref[0] == 0
    sums = []
    for part in range(2):
        sums.append(dot(table_ref[...], src_ref[:, part].reshape(GY * 64, NX)))
    sums.append(dot(table_ref[...], extra_ref[...].reshape(GY * 64, NX)))
    zero = jnp.zeros((128, NX), F32)
    cc, cs = sums[0][:128], sums[0][128:]
    sc, ss = sums[1][:128], sums[1][128:]
    ec, es = sums[2][:128], sums[2][128:]
    pc, ps = jnp.where(first, zero, sc), jnp.where(first, zero, ss)
    nc, ns = jnp.where(first, sc, cc), jnp.where(first, ss, cs)
    mc, ms = jnp.where(first, ec, -sc), jnp.where(first, es, -ss)
    parts = (cc - ps, -(cs + pc), nc - ms, -(ns + mc))
    for index, part in enumerate(parts):
        out_ref[:, index] = part.astype(BF16).reshape(GZ, 16, NX)


def y_transform(first, rows, extra):
    return pl.pallas_call(
        y_kernel,
        in_specs=[
            pl.BlockSpec(memory_space=pltpu.SMEM),
            pl.BlockSpec(memory_space=pltpu.VMEM),
            pl.BlockSpec(memory_space=pltpu.VMEM),
            pl.BlockSpec(memory_space=pltpu.VMEM),
        ],
        out_specs=pl.BlockSpec(memory_space=pltpu.VMEM),
        out_shape=jax.ShapeDtypeStruct((GZ, 4, 16, NX), BF16),
        compiler_params=params(),
        name="y_transform",
    )(first, rows, extra, const(tables()[2]))


def y_back_kernel(first_ref, src_ref, table_ref, out_ref, extra_ref):
    first = first_ref[0] == 0
    ar, ai, br, bi = [
        src_ref[:, part].reshape(128, NX).astype(F32) for part in range(4)
    ]
    rows = (
        (jnp.where(first, ar, ar + br), jnp.where(first, -ai, -(ai + bi))),
        (jnp.where(first, br, bi - ai), jnp.where(first, -bi, br - ar)),
        (jnp.where(first, -bi, 0.0), jnp.where(first, -br, 0.0)),
    )
    for part, (upper, lower) in enumerate(rows):
        operand = jnp.concatenate([upper, lower], axis=0).astype(BF16)
        result = dot(table_ref[...], operand).astype(BF16).reshape(GY, 64, NX)
        if part < 2:
            out_ref[:, part] = result
        else:
            extra_ref[...] = result


def y_back(first, modes):
    return pl.pallas_call(
        y_back_kernel,
        in_specs=[
            pl.BlockSpec(memory_space=pltpu.SMEM),
            pl.BlockSpec(memory_space=pltpu.VMEM),
            pl.BlockSpec(memory_space=pltpu.VMEM),
        ],
        out_specs=[pl.BlockSpec(memory_space=pltpu.VMEM)] * 2,
        out_shape=[
            jax.ShapeDtypeStruct((GY, 2, 64, NX), BF16),
            jax.ShapeDtypeStruct((GY, 64, NX), BF16),
        ],
        compiler_params=params(),
        name="y_back",
    )(first, modes, const(tables()[2].T))


def z_kernel(factor, src_ref, table_ref, out_ref):
    for m in range(2):
        sums = []
        for p in range(2):
            block = src_ref[:, m * 2 + p].reshape(128, NX)
            pair = []
            for t in range(2):
                total = None
                for inner in range(4):
                    term = dot(table_ref[t, inner], block[:, inner * C : inner * C + C])
                    total = term if total is None else total + term
                pair.append(total)
            sums.append(pair)
        real = sums[0][0] + sums[1][1]
        imag = sums[1][0] - sums[0][1]
        out_ref[:, :, m * 128 : m * 128 + 128] = (
            jnp.concatenate([real, imag], axis=1) * factor
        ).reshape(GY, 8, 128)


def z_transform(modes, factor):
    return pl.pallas_call(
        functools.partial(z_kernel, factor),
        in_specs=[pl.BlockSpec(memory_space=pltpu.VMEM)] * 2,
        out_specs=pl.BlockSpec(memory_space=pltpu.VMEM),
        out_shape=jax.ShapeDtypeStruct((GY, 8, 256), F32),
        compiler_params=params(),
        name="z_transform",
    )(modes, const(tables()[3]))


def z_back_kernel(src_ref, table_ref, out_ref):
    for m in range(2):
        block = src_ref[:, :, m * 128 : m * 128 + 128].reshape(128, 128).astype(BF16)
        real, imag = [], []
        for inner in range(4):
            cos_part = dot(table_ref[0, inner], block)
            sin_part = dot(table_ref[1, inner], block)
            real.append(cos_part[:, :C] - sin_part[:, C:])
            imag.append(cos_part[:, C:] + sin_part[:, :C])
        for p, pieces in enumerate((real, imag)):
            full = jnp.concatenate(pieces, axis=1).astype(BF16)
            out_ref[:, m * 2 + p] = full.reshape(GZ, 16, NX)


def z_back(modes):
    return pl.pallas_call(
        z_back_kernel,
        in_specs=[pl.BlockSpec(memory_space=pltpu.VMEM)] * 2,
        out_specs=pl.BlockSpec(memory_space=pltpu.VMEM),
        out_shape=jax.ShapeDtypeStruct((GZ, 4, 16, NX), BF16),
        compiler_params=params(),
        name="z_back",
    )(modes, const(tables()[3].transpose(0, 1, 3, 2)))


def to_kx(dealt):
    split = dealt.reshape(GY, 4, 2, 2, 2, C)
    plus, minus = split[:, :, :, 0], split[:, :, :, 1]
    order = jnp.concatenate([plus, minus[:1], minus[1:][::-1]], axis=0)
    return order.transpose(1, 2, 0, 3, 4)


def from_kx(modes):
    order = modes.transpose(2, 0, 1, 3, 4)
    minus = jnp.concatenate([order[16:17], order[17:][::-1]], axis=0)
    return jnp.stack([order[:16], minus], axis=3).reshape(GY, 8, 256)


def weight_grad_kernel(u_ref, g_ref, mask_ref, out_ref):
    for block in range(4):
        right = jnp.concatenate([g_ref[block]] * 8, axis=1) * mask_ref[...]
        result = dot(u_ref[block], right, TN)
        for mode in range(8):
            out_ref[0, block * 8 + mode] = result[:, mode * 128 : mode * 128 + 128]


def weight_grad(modes_in, grad_modes):
    u = modes_in.reshape(M, 16, C)
    real, imag = grad_modes[..., 0, :], grad_modes[..., 1, :]
    g = jnp.stack(
        [jnp.concatenate([real, imag], axis=-1), jnp.concatenate([imag, -real], axis=-1)], axis=3
    ).reshape(M, 16, 128)
    mask = const(np.kron(np.eye(8), np.ones((2, 128))))
    return pl.pallas_call(
        weight_grad_kernel,
        grid=(8,),
        in_specs=[
            pl.BlockSpec((4, 16, C), lambda i: (i, 0, 0)),
            pl.BlockSpec((4, 16, 128), lambda i: (i, 0, 0)),
            whole((16, 1024)),
        ],
        out_specs=pl.BlockSpec((1, M, C, 128), lambda i: (i, 0, 0, 0)),
        out_shape=jax.ShapeDtypeStruct((8, M, C, 128), F32),
        compiler_params=params(),
        name="weight_grad",
    )(u, g, mask)


def normal_parts(value):
    size = jnp.abs(value)
    decay = jnp.exp(-0.5 * value * value)
    t = 1.0 / (1.0 + TAIL_SCALE * size)
    poly = jnp.full_like(value, TAIL[-1])
    for coefficient in TAIL[-2::-1]:
        poly = poly * t + coefficient
    tail = poly * t * decay
    return jnp.where(value < 0.0, tail, 1.0 - tail), decay * (1.0 / math.sqrt(2.0 * math.pi))


def dense_kernel(
    rows_ref, odd_ref, cells_ref, table_ref, point_ref, bias_ref, out_w_ref, out_b_ref,
    hidden_ref, slope_ref, field_ref, low_ref, high_ref, corner_ref, rows,
):
    y = pl.program_id(0)

    @pl.when(y == 0)
    def _():
        corner_ref[...] = jnp.zeros_like(corner_ref)
        for half in range(2):
            lanes = slice(half * 128, half * 128 + 128)
            for g in range(GY * 2):
                rows[half, g * 64 : g * 64 + 64, :] = rows_ref[g, :, lanes].astype(F32)
            rows[half, 2048:2112, :] = odd_ref[:, lanes].astype(F32)
            rows[half, 2112:2560, :] = jnp.zeros((448, 128), F32)

    def quad(q, carry):
        picked = jnp.concatenate(
            [rows[half, pl.ds(y * QZ + q, 40, stride=64), :] for half in range(2)], axis=1
        ).astype(BF16)
        spectral = dot(picked, table_ref[...], TN)
        for inner in range(4):
            z = q * 4 + inner
            pre = (
                spectral[inner * C : inner * C + C]
                + dot(point_ref[...], cells_ref[0, z])
                + bias_ref[...]
            )
            normal_cdf, density = normal_parts(pre)
            hidden = (pre * normal_cdf).astype(BF16)
            hidden_ref[0, z] = hidden
            slope_ref[0, z] = (normal_cdf + pre * density).astype(BF16)
            b_rows = dot(out_w_ref[...], hidden)
            for b in range(3):
                field_ref[b, 0, pl.ds(z, 1), :] = b_rows[b : b + 1] + out_b_ref[b]
        return carry

    lax.fori_loop(0, QZ, quad, 0)
    for b in range(3):
        for i in range(2):
            z = LZ - 2 + i
            low_ref[b, pl.ds(y * 2 + i, 1), :] = field_ref[b, 0, i : i + 1, :]
            high_ref[b, pl.ds(y * 2 + i, 1), :] = field_ref[b, 0, z : z + 1, :]
    for y_edge in range(2):

        @pl.when(y == y_edge * (LY - 1))
        def _(y_edge=y_edge):
            for b in range(3):
                for z_edge in range(2):
                    z = z_edge * (LZ - 1)
                    corner_ref[y_edge * 2 + z_edge, b : b + 1, :] = field_ref[b, 0, z : z + 1, :]


def dense(rows, odd, cells, point_weight, point_bias, out_weight, out_bias):
    out_w = jnp.pad(out_weight.T, ((0, 5), (0, 0)))
    cell_spec = pl.BlockSpec((1, LZ, C, NX), lambda y: (y, 0, 0, 0))
    cell_shape = jax.ShapeDtypeStruct((LY, LZ, C, NX), BF16)
    return pl.pallas_call(
        dense_kernel,
        grid=(LY,),
        in_specs=[
            whole((GY * 2, 64, NX)),
            whole((64, NX)),
            cell_spec,
            whole((40, NX)),
            whole((C, C)),
            whole((C, 1)),
            whole((8, C)),
            pl.BlockSpec(memory_space=pltpu.SMEM),
        ],
        out_specs=[
            cell_spec,
            cell_spec,
            pl.BlockSpec((3, 1, LZ, NX), lambda y: (0, y, 0, 0)),
            whole((3, 32, NX)),
            whole((3, 32, NX)),
            whole((4, 8, NX)),
        ],
        out_shape=[
            cell_shape,
            cell_shape,
            jax.ShapeDtypeStruct((3, LY, LZ, NX), F32),
            jax.ShapeDtypeStruct((3, 32, NX), F32),
            jax.ShapeDtypeStruct((3, 32, NX), F32),
            jax.ShapeDtypeStruct((4, 8, NX), F32),
        ],
        scratch_shapes=[pltpu.VMEM((2, 40 * 64, 128), F32)],
        compiler_params=params(),
        name="dense",
    )(
        rows.reshape(GY * 2, 64, NX),
        odd,
        cells,
        const(tables()[1]),
        point_weight.T,
        point_bias[:, None],
        out_w,
        out_bias,
    )


def grad_kernel(
    hidden_ref, slope_ref, cells_ref, grad_ref, table_ref, out_w_ref,
    rows_ref, odd_ref, point_ref, bias_ref, out_ref,
    stage, rows, point_sum, bias_sum, out_sum,
):
    y = pl.program_id(0)

    @pl.when(y == 0)
    def _():
        point_sum[...] = jnp.zeros_like(point_sum)
        bias_sum[...] = jnp.zeros_like(bias_sum)
        out_sum[...] = jnp.zeros_like(out_sum)

    def quad(q, carry):
        for inner in range(4):
            z = q * 4 + inner
            grad = jnp.concatenate(
                [grad_ref[b, 0, pl.ds(z, 1), :] for b in range(3)] + [jnp.zeros((5, NX), F32)],
                axis=0,
            )
            upper = grad.astype(BF16)
            lower = (grad - upper.astype(F32)).astype(BF16)
            both = jnp.concatenate([upper, lower], axis=0)
            grad_hidden = dot(out_w_ref[...], both)
            stage[inner * C : inner * C + C, :] = (
                grad_hidden * slope_ref[0, z].astype(F32)
            ).astype(BF16)
            out_sum[...] += dot(both, hidden_ref[0, z], NT)
        block = stage[...]
        x_rows = dot(table_ref[...], block, NT)
        put_rows(rows, y * QZ + q, x_rows)
        bias_sum[...] += x_rows[0:8]
        cells = cells_ref[0, pl.ds(q * 4, 4)].reshape(4 * C, NX)
        point_sum[...] += dot(cells, block, NT)
        return carry

    lax.fori_loop(0, QZ, quad, 0)

    @pl.when(y == LY - 1)
    def _():
        emit_rows(rows, rows_ref, odd_ref)
        total = point_sum[0:C, 0:C]
        bias = bias_sum[0:1, 0:C]
        for inner in range(1, 4):
            span = slice(inner * C, inner * C + C)
            total = total + point_sum[span, span]
            bias = bias + bias_sum[0:1, span]
        point_ref[...] = total
        bias_ref[...] = bias
        out_ref[...] = out_sum[0:8] + out_sum[8:16]


def grad_dense(hidden, slope, cells, grad_b, out_weight):
    forward = const(tables()[0])
    out_w = jnp.pad(out_weight, ((0, 0), (0, 5)))
    out_w = jnp.concatenate([out_w, out_w], axis=1)
    cell_spec = pl.BlockSpec((1, LZ, C, NX), lambda y: (y, 0, 0, 0))
    return pl.pallas_call(
        grad_kernel,
        grid=(LY,),
        in_specs=[
            cell_spec,
            cell_spec,
            cell_spec,
            pl.BlockSpec((3, 1, LZ, NX), lambda y: (0, y, 0, 0)),
            whole((40, NX)),
            whole((C, 16)),
        ],
        out_specs=[
            whole((GY, 2, 64, NX)),
            whole((64, NX)),
            whole((C, C)),
            whole((1, C)),
            whole((8, C)),
        ],
        out_shape=[
            jax.ShapeDtypeStruct((GY, 2, 64, NX), BF16),
            jax.ShapeDtypeStruct((64, NX), BF16),
            jax.ShapeDtypeStruct((C, C), F32),
            jax.ShapeDtypeStruct((1, C), F32),
            jax.ShapeDtypeStruct((8, C), F32),
        ],
        scratch_shapes=[
            pltpu.VMEM((4 * C, NX), BF16),
            pltpu.VMEM((2, 40 * 64, 128), F32),
            pltpu.VMEM((4 * C, 4 * C), F32),
            pltpu.VMEM((8, NX), F32),
            pltpu.VMEM((16, C), F32),
        ],
        compiler_params=params(),
        name="grad_dense",
    )(hidden, slope, cells, grad_b, forward, out_w)


DIRECTIONS = [(dy, dz) for dy in (-1, 0, 1) for dz in (-1, 0, 1) if dy or dz]


def halo_kernel(
    field, low, high, corner, y_low, y_high, z_low, z_high, corner_out, send, recv
):
    g, h = lax.axis_index("gy"), lax.axis_index("gz")

    def piece(dy, dz):
        if dz == 0:
            start = LY - 2 if dy > 0 else 0
            return field.at[:, pl.ds(start, 2)], (y_low if dy > 0 else y_high)
        if dy == 0:
            return (high, z_low) if dz > 0 else (low, z_high)
        index = (2 if dy > 0 else 0) + (1 if dz > 0 else 0)
        return corner.at[index], corner_out.at[3 - index]

    def exists(dy, dz):
        y, z = g + dy, h + dz
        return jnp.logical_and(
            jnp.logical_and(y >= 0, y < GY), jnp.logical_and(z >= 0, z < GZ)
        )

    def copy(index):
        dy, dz = DIRECTIONS[index]
        src, dst = piece(dy, dz)
        return pltpu.make_async_remote_copy(
            src_ref=src, dst_ref=dst, send_sem=send.at[index], recv_sem=recv.at[index],
            device_id={"gy": g + dy, "gz": h + dz}, device_id_type=MESH,
        )

    barrier = pltpu.get_barrier_semaphore()
    for dy, dz in DIRECTIONS:

        @pl.when(exists(dy, dz))
        def _(dy=dy, dz=dz):
            pl.semaphore_signal(
                barrier, inc=1, device_id={"gy": g + dy, "gz": h + dz}, device_id_type=MESH
            )

    y_sides = jnp.where(g > 0, 1, 0) + jnp.where(g < GY - 1, 1, 0)
    z_sides = jnp.where(h > 0, 1, 0) + jnp.where(h < GZ - 1, 1, 0)
    pl.semaphore_wait(barrier, (y_sides + 1) * (z_sides + 1) - 1)
    for index in range(8):

        @pl.when(exists(*DIRECTIONS[index]))
        def _(index=index):
            copy(index).start()

    for index in range(8):
        dy, dz = DIRECTIONS[index]

        @pl.when(exists(dy, dz))
        def _(index=index):
            copy(index).wait_send()

        @pl.when(exists(-dy, -dz))
        def _(index=index):
            copy(index).wait_recv()


def halo(collective_id, field, low, high, corner):
    side = jax.ShapeDtypeStruct((3, 2, LZ, NX), F32)
    edge = jax.ShapeDtypeStruct((3, 32, NX), F32)
    return pl.pallas_call(
        halo_kernel,
        out_shape=[side, side, edge, edge, jax.ShapeDtypeStruct((4, 8, NX), F32)],
        in_specs=[ANY] * 4,
        out_specs=[ANY] * 5,
        scratch_shapes=[pltpu.SemaphoreType.DMA((8,))] * 2,
        compiler_params=pltpu.CompilerParams(
            collective_id=collective_id, has_side_effects=True
        ),
        name="halo",
    )(field, low, high, corner)


def cell_loss(field_b, slope_x, slope_y, slope_z):
    current_x = slope_y[2] - slope_z[1]
    current_y = slope_z[0] - slope_x[2]
    current_z = slope_x[1] - slope_y[0]
    force_x = current_y * field_b[2] - current_z * field_b[1]
    force_y = current_z * field_b[0] - current_x * field_b[2]
    force_z = current_x * field_b[1] - current_y * field_b[0]
    spread = slope_x[0] + slope_y[1] + slope_z[2]
    strength = field_b[0] * field_b[0] + field_b[1] * field_b[1] + field_b[2] * field_b[2] + 1.0
    return (force_x * force_x + force_y * force_y + force_z * force_z) / strength + spread * spread


def stencil_kernel(
    place_ref, field_ref, y_low_ref, y_high_ref, z_low_ref, z_high_ref, corner_ref,
    grad_ref, loss_ref, bias_ref, wide, own, slopes,
):
    g, h = place_ref[0], place_ref[1]
    zero_rows = jnp.zeros((8, NX), F32)

    def kept(present, value):
        return jnp.where(present, value, jnp.zeros_like(value))

    for b in range(3):
        wide[b, 2:18, 8:24, :] = field_ref[b]
        wide[b, 0:2, 8:24, :] = kept(g > 0, y_low_ref[b])
        wide[b, 18:20, 8:24, :] = kept(g < GY - 1, y_high_ref[b])
        for plane in (0, 1, 18, 19):
            wide[b, plane, 0:8, :] = zero_rows
            wide[b, plane, 24:32, :] = zero_rows
        for y in range(LY):
            wide[b, y + 2, 0:8, :] = zero_rows
            wide[b, y + 2, 24:32, :] = zero_rows
            wide[b, y + 2, 6:8, :] = kept(h > 0, z_low_ref[b, 2 * y : 2 * y + 2, :])
            wide[b, y + 2, 24:26, :] = kept(h < GZ - 1, z_high_ref[b, 2 * y : 2 * y + 2, :])
        for index in range(4):
            y_side = g < GY - 1 if index // 2 else g > 0
            z_side = h < GZ - 1 if index % 2 else h > 0
            row = 24 if index % 2 else 7
            wide[b, 18 if index // 2 else 1, row : row + 1, :] = kept(
                jnp.logical_and(y_side, z_side), corner_ref[index, b : b + 1, :]
            )
    lane = lax.broadcasted_iota(jnp.int32, (32, NX), 1)
    row = lax.broadcasted_iota(jnp.int32, (32, NX), 0)
    z_cell = h * LZ + row - 8
    weight = jnp.where((z_cell >= 0) & (z_cell < NZ), 1.0 / CELLS, 0.0).astype(F32)
    inner = (row >= 8) & (row < 24)

    def x_diff(value):
        after = jnp.where(lane == NX - 1, 0.0, pltpu.roll(value, NX - 1, 1))
        before = jnp.where(lane == 0, 0.0, pltpu.roll(value, 1, 1))
        return (after - before) * 0.5

    def z_diff(value):
        return (pltpu.roll(value, 31, 0) - pltpu.roll(value, 1, 0)) * 0.5

    def one(plane, loss):
        cells = tuple(wide[b, plane] for b in range(3))
        slope_x = tuple(x_diff(value) for value in cells)
        slope_y = tuple((wide[b, plane + 1] - wide[b, plane - 1]) * 0.5 for b in range(3))
        slope_z = tuple(z_diff(value) for value in cells)
        terms, pullback = jax.vjp(cell_loss, cells, slope_x, slope_y, slope_z)
        y_cell = g * LY + plane - 2
        y_inside = jnp.logical_and(y_cell >= 0, y_cell < NY)
        grad_own, grad_x, grad_y, grad_z = pullback(jnp.where(y_inside, weight, 0.0))
        for b in range(3):
            own[b, plane - 1] = grad_own[b] - x_diff(grad_x[b]) - z_diff(grad_z[b])
            slopes[b, plane - 1] = grad_y[b]
        counted = jnp.logical_and(plane >= 2, plane < 18)
        return loss + jnp.where(jnp.logical_and(inner, counted), terms, 0.0)

    loss = lax.fori_loop(1, 19, one, jnp.zeros((32, NX), F32))
    loss_ref[...] = loss

    def finish(y, sums):
        result = []
        for b in range(3):
            grad = own[b, y + 1, 8:24, :] + (
                slopes[b, y, 8:24, :] - slopes[b, y + 2, 8:24, :]
            ) * 0.5
            grad_ref[b, y] = grad
            result.append(sums[b] + grad)
        return tuple(result)

    sums = lax.fori_loop(0, LY, finish, tuple(jnp.zeros((LZ, NX), F32) for _ in range(3)))
    for b in range(3):
        bias_ref[b] = sums[b]


def stencil(place, field, *halos):
    vmem = pl.BlockSpec(memory_space=pltpu.VMEM)
    return pl.pallas_call(
        stencil_kernel,
        in_specs=[pl.BlockSpec(memory_space=pltpu.SMEM)] + [vmem] * 6,
        out_specs=[vmem] * 3,
        out_shape=[
            jax.ShapeDtypeStruct((3, LY, LZ, NX), F32),
            jax.ShapeDtypeStruct((32, NX), F32),
            jax.ShapeDtypeStruct((3, LZ, NX), F32),
        ],
        scratch_shapes=[
            pltpu.VMEM((3, 20, 32, NX), F32),
            pltpu.VMEM((3, 18, 32, NX), F32),
            pltpu.VMEM((3, 18, 32, NX), F32),
        ],
        compiler_params=params(),
        name="stencil",
    )(place, field, *halos)


def on_device(field_in, spectral_weight, point_weight, point_bias, out_weight, out_bias):
    first = lax.axis_index("gy").astype(jnp.int32).reshape(1)
    place = jnp.stack([lax.axis_index("gy"), lax.axis_index("gz")]).astype(jnp.int32)
    cells, rows, odd = x_transform(field_in)
    rows, odd = swap("gy", GY, 1, ("swap", rows), ("to0", odd))
    modes = swap("gz", GZ, 2, ("swap", y_transform(first, rows, odd)))
    modes_in = to_kx(deal(False, 3, z_transform(modes, SCALE)).astype(BF16))

    mixed = jnp.einsum(
        "abkpi,abkio->abkpo", modes_in, spectral_weight, preferred_element_type=F32
    )
    real = mixed[..., 0, :C] - mixed[..., 1, C:]
    imag = mixed[..., 0, C:] + mixed[..., 1, :C]
    modes_out = jnp.stack([real, imag], axis=3)

    back = z_back(deal(True, 4, from_kx(modes_out)))
    rows, odd = y_back(first, swap("gz", GZ, 5, ("swap", back)))
    rows, odd = swap("gy", GY, 6, ("swap", rows), ("from0", odd))

    hidden, slope, field_b, *edges = dense(
        rows, odd, cells, point_weight, point_bias, out_weight, out_bias
    )
    grad_b, loss_rows, bias_rows = stencil(place, field_b, *halo(10, field_b, *edges))
    rows, odd, point_part, point_bias_part, out_part = grad_dense(
        hidden, slope, cells, grad_b, out_weight
    )
    small = jnp.concatenate(
        [
            jnp.sum(loss_rows).reshape(1),
            jnp.sum(bias_rows, axis=(1, 2)),
            point_bias_part[0],
            out_part[:3].reshape(-1),
        ]
    )
    small = jnp.concatenate(
        [point_part.reshape(32, 128), jnp.pad(small, (0, 1024 - 260)).reshape(8, 128)]
    )
    rows, odd, small = swap("gy", GY, 7, ("swap", rows), ("to0", odd), ("all", small))
    modes, small = swap(
        "gz", GZ, 8, ("swap", y_transform(first, rows, odd)), ("all", jnp.sum(small, axis=0))
    )
    small = jnp.sum(small, axis=0)
    grad_modes = to_kx(deal(False, 9, z_transform(modes, 1.0)).astype(BF16))
    grad_spectral = weight_grad(modes_in, grad_modes).reshape(4, 2, M, C, 2 * C)
    grad_point = small[:32].reshape(C, C)
    rest = small[32:].reshape(-1)
    return (
        rest[0] / CELLS,
        grad_spectral,
        grad_point,
        rest[4:68],
        rest[68:260].reshape(3, C).T,
        rest[1:4],
    )


def solution(mesh):
    return jax.shard_map(
        on_device,
        mesh=mesh,
        in_specs=(P(None, "gy", "gz", None), P("gz", "gy", None, None, None), P(), P(), P(), P()),
        out_specs=(P(), P("gz", "gy", None, None, None), P(), P(), P(), P()),
        check_vma=False,
    )
```

time: 790 us -> 299 us (0.38)
  waiting for transfers between devices: 318 us -> 0 us
  Pallas kernels: 0 us -> 273 us
  other arithmetic: 183 us -> 8.93 us
  matrix products: 106 us -> 3.37 us
  blocking collectives: 89.6 us -> 0 us
  local copies, waits for them, and re-layouts: 59.1 us -> 9.89 us
  between operations: 16.3 us -> 2.78 us
  starting transfers between devices: 8.05 us -> 0 us
    pallas_call x0 -> x21, Pallas kernels: none -> 273 us  [the longest x6 109 us: swap(): pl.pallas_call(functools.partial(swap_kernel, axis, count, modes), out_sh...]
    reduce_scatter x4 -> x0, waiting for transfers between devices: 244 us -> none  [the longest x2 209 us: to_modes(): lax.psum_scatter(rotate(with_cos, with_sin, True), 'gy', scatter_dimensio...]
    dot_general x21 -> x1, matrix products: 106 us -> 3.37 us  [on_device(): jnp.einsum('abkpi,abkio->abkpo', modes_in, spectral_weight, preferred_ele...]
    psum x1 -> x0, blocking collectives: 66.3 us -> none  [on_device(): lax.psum((loss_local, point_part, point_bias_part, out_part, out_bias_par...]
    all_gather x1 -> x0, waiting for transfers between devices: 65.5 us -> none  [from_modes(): portion = lax.all_gather(z_back, 'gy', axis=0, tiled=True)]
    add x7 -> x0, other arithmetic: 58.5 us -> none  [the longest x4 38.6 us: rotate(): return jnp.concatenate([cos_real + sin_imag, cos_imag - sin_real], axis=-1)]
    convert_element_type x7 -> x2, other arithmetic: 42.5 us -> 1.83 us  [the longest x1 0.91 us: on_device(): modes_in = to_kx(deal(False, 3, z_transform(modes, SCALE)).astype(BF16))]
    concatenate x11 -> x3, other arithmetic: 39.7 us -> 1.49 us  [the longest x1 0.87 us: to_kx(): order = jnp.concatenate([plus, minus[:1], minus[1:][::-1]], axis=0)]
  transfers between devices with their start and end apart: 9 -> 0, of which waited for: 7 -> 0; matrix products, arithmetic and copies ran while one was open for 3% -> 0% of each run, Pallas kernels for 0% -> 0%
where the time goes in v1:
time: 299 us; the launch traced here: 298 us
  Pallas kernels  273 us (91%)
  local copies, waits for them, and re-layouts  9.89 us (3%)
  other arithmetic  8.93 us (3%)
  matrix products  3.37 us (1%)
    pallas_call x6, Pallas kernels, swap(): pl.pallas_call(functools.partial(swap_kernel, axis, count, modes), out_sh...  109 us
    pallas_call x1, Pallas kernels, dense(): pl.pallas_call(dense_kernel, grid=(LY,), in_specs=[whole((GY * 2, 64, NX)...  45.8 us
    pallas_call x3, Pallas kernels, deal(): pl.pallas_call(functools.partial(deal_kernel, inward), out_shape=jax.Shap...  31.5 us
    pallas_call x1, Pallas kernels, grad_dense(): pl.pallas_call(grad_kernel, grid=(LY,), in_specs=[cell_spec, cell_spec, c...  30.3 us
    pallas_call x1, Pallas kernels, x_transform(): pl.pallas_call(x_kernel, grid=(LY,), in_specs=[pl.BlockSpec((C, 1, LZ, NX...  18.1 us
    pallas_call x1, Pallas kernels, halo(): pl.pallas_call(halo_kernel, out_shape=[side, side, edge, edge, jax.ShapeD...  8.43 us
    pallas_call x1, Pallas kernels, stencil(): pl.pallas_call(stencil_kernel, in_specs=[pl.BlockSpec(memory_space=pltpu....  7.26 us
    pallas_call x1, Pallas kernels, weight_grad(): pl.pallas_call(weight_grad_kernel, grid=(8,), in_specs=[pl.BlockSpec((4,...  6.76 us

profile of v1, /device:TPU:1, one launch (start us, length us, event | category | flops | bytes accessed | tf_op | source)
XLA Modules:
  0.0 297.5 jit_solution(10024579185736434207)
XLA Ops:
  0.6 18.1 %x_transform.1 = (bf16[16,16,64,256]{3,2,1,0:T(8,128)(2,1)}, bf16[16,2,64,256]{3,2,1,0:T(8,128)(2,1)}, bf16[64,256]{1,0:T(8,128)(2,1)}) custom-call(bf16[64,16,16,256]{3,2,1,0:T(8,128)(2,1)} %field_ref.1, bf16[40,256]{1,0:T(8,128)(2,1)} %constant.33.clone.table_ref), custom_call_target="tpu_custom_call" | custom-call | tf_op jit(solution)/shard_map/x_transform/pallas_call | solution.py:303
  18.7 26.1 %swap_1.1 = (bf16[16,2,64,256]{3,2,1,0:T(8,128)(2,1)}, bf16[16,64,256]{2,1,0:T(8,128)(2,1)}) custom-call(bf16[16,2,64,256]{3,2,1,0:T(8,128)(2,1)} %get-tuple-element.39.refs_0_, bf16[64,256]{1,0:T(8,128)(2,1)} %get-tuple-element.40.refs_1_), custom_call_target="tpu_custom_call" | custom-call | tf_op jit(solution)/shard_map/swap_1/pallas_call | solution.py:175
  44.9 2.8 y_transform.2.refs_0_
  47.7 8.3 %swap_2.1.src_ref = bf16[8,4,16,256]{3,2,1,0:T(8,128)(2,1)} custom-call(bf16[8,4,16,256]{3,2,1,0:T(8,128)(2,1)} %y_transform.2.refs_0_), custom_call_target="tpu_custom_call" | custom-call | tf_op jit(solution)/shard_map/swap_2/pallas_call | solution.py:175
  56.0 2.2 z_transform.2.src
  58.3 9.9 %deal_3.1 = f32[16,8,256]{2,1,0:T(8,128)} custom-call(f32[16,8,256]{2,1,0:T(8,128)} %z_transform.2.src), custom_call_target="tpu_custom_call" | custom-call | tf_op jit(solution)/shard_map/deal_3/pallas_call | solution.py:257
  69.5 3.4 %fusion = f32[4,2,32,2,128]{4,3,2,1,0:T(2,128)S(1)} fusion(bf16[4,2,32,64,128]{4,3,2,1,0:T(8,128)(2,1)} %param.17, bf16[15,4,2,2,64]{4,3,0,2,1:T(2,128)(2,1)S(1)} %rev.9, bf16[1,4,2,2,64]{4,3,0,2,1:T(2,128)(2,1)S(1)} %slice_bitcast_fusion.5, bf16[16,4,2,2,64]{4,3,0,2,1:T(2,128)(2,1)S(1)} %copy_bitcast_fusion.2), kind=kOutput, calls=%fused_computation.9 | convolution fusion | flops 8585216 | bytes 4521984 | tf_op jit(solution)/shard_map/abkpi,abkio->abkpo/dot_general | solution.py:896
  75.1 10.9 %deal_4.1.src_ref = f32[16,8,256]{2,1,0:T(8,128)} custom-call(f32[16,8,256]{2,1,0:T(8,128)} %reshape.65.src), custom_call_target="tpu_custom_call" | custom-call | tf_op jit(solution)/shard_map/deal_4/pallas_call | solution.py:257
  86.0 2.2 z_back.1.refs_0_
  88.2 14.6 %swap_5.1.src_ref = bf16[8,4,16,256]{3,2,1,0:T(8,128)(2,1)} custom-call(bf16[8,4,16,256]{3,2,1,0:T(8,128)(2,1)} %z_back.1.refs_0_), custom_call_target="tpu_custom_call" | custom-call | tf_op jit(solution)/shard_map/swap_5/pallas_call | solution.py:175
  102.8 2.9 y_back.1
  105.7 18.9 %swap_6.1 = (bf16[16,2,64,256]{3,2,1,0:T(8,128)(2,1)}, bf16[64,256]{1,0:T(8,128)(2,1)}) custom-call(bf16[16,2,64,256]{3,2,1,0:T(8,128)(2,1)} %get-tuple-element.43.refs_0_, bf16[16,64,256]{2,1,0:T(8,128)(2,1)} %get-tuple-element.44.refs_1_), custom_call_target="tpu_custom_call" | custom-call | tf_op jit(solution)/shard_map/swap_6/pallas_call | solution.py:175
  126.6 45.8 %dense.1 = (bf16[16,16,64,256]{3,2,1,0:T(8,128)(2,1)}, bf16[16,16,64,256]{3,2,1,0:T(8,128)(2,1)}, f32[3,16,16,256]{3,2,1,0:T(8,128)}, f32[3,32,256]{2,1,0:T(8,12...) custom-call(bf16[32,64,256]{2,1,0:T(8,128)(2,1)} %bitcast.59, bf16[64,256]{1,0:T(8,128)(2,1)} %get-tuple-element.46.odd_ref, ...), custom_call_target="tpu_custom_call" | custom-call | tf_op jit(solution)/shard_map/dense/pallas_call | solution.py:564
  172.4 8.4 %halo.1 = (f32[3,2,16,256]{3,2,1,0:T(8,128)}, f32[3,2,16,256]{3,2,1,0:T(8,128)}, f32[3,32,256]{2,1,0:T(8,128)}, f32[3,32,256]{2,1,0:T(8,128)}, f32[4,8,256]{2,1,0:T(8,128)}) custom-call(f32[3,16,16,256]{3,2,1,0:T(8,128)} %get-tuple-element.50.field.field_ref, f32[3,32,256]{2,1,0:T(8,128)} %get-tuple-element.51.low, f32[3,32,256]{2,1,0:T(8,128)} %get-tuple-element.52.high, ...), custom_call_target="tpu_custom_call" | custom-call | tf_op jit(solution)/shard_map/halo/pallas_call | solution.py:766
  181.4 7.3 %stencil.1 = (f32[3,16,16,256]{3,2,1,0:T(8,128)}, f32[32,256]{1,0:T(8,128)}, f32[3,16,256]{2,1,0:T(8,128)}) custom-call(s32[2]{0:T(128)} %pad_add_fusion.place_ref, f32[3,16,16,256]{3,2,1,0:T(8,128)} %get-tuple-element.50.field.field_ref, f32[3,2,16,256]{3,2,1,0:T(8,128)} %get-tuple-element.54.y_low_ref, f32[3,2,16,256]{3,2,1,0:T(8,128)} %get-tuple-element.55.y_high_ref, ...), custom_call_target="tpu_custom_call" | custom-call | tf_op jit(solution)/shard_map/stencil/pallas_call | solution.py:869
  189.4 30.3 %grad_dense.1 = (bf16[16,2,64,256]{3,2,1,0:T(8,128)(2,1)}, bf16[64,256]{1,0:T(8,128)(2,1)}, f32[64,64]{1,0:T(8,128)}, f32[1,64]{1,0:T(1,128)}, f32[8,64]{1,0:T(8,128)}) custom-call(bf16[16,16,64,256]{3,2,1,0:T(8,128)(2,1)} %get-tuple-element.48.hidden_ref, bf16[16,16,64,256]{3,2,1,0:T(8,128)(2,1)} %get-tuple-element.49.slope_ref, ...), custom_call_target="tpu_custom_call" | custom-call | tf_op jit(solution)/shard_map/grad_dense/pallas_call | solution.py:665
  222.0 1.4 fusion.2
  224.0 31.8 %swap_7.1 = (bf16[16,2,64,256]{3,2,1,0:T(8,128)(2,1)}, bf16[16,64,256]{2,1,0:T(8,128)(2,1)}, f32[16,40,128]{2,1,0:T(8,128)}) custom-call(bf16[16,2,64,256]{3,2,1,0:T(8,128)(2,1)} %get-tuple-element.60.refs_0_, bf16[64,256]{1,0:T(8,128)(2,1)} %get-tuple-element.61.refs_1_, f32[40,128]{1,0:T(8,128)} %pad_maximum_fusion.3.refs_2_), custom_call_target="tpu_custom_call" | custom-call | tf_op jit(solution)/shard_map/swap_7/pallas_call | solution.py:175
  255.9 2.8 y_transform.3.refs_0_
  258.7 1.6 reduce_sum.38.refs_1_
  260.3 9.4 %swap_8.1 = (bf16[8,4,16,256]{3,2,1,0:T(8,128)(2,1)}, f32[8,40,128]{2,1,0:T(8,128)}) custom-call(bf16[8,4,16,256]{3,2,1,0:T(8,128)(2,1)} %y_transform.3.refs_0_, f32[40,128]{1,0:T(8,128)} %reduce_sum.38.refs_1_), custom_call_target="tpu_custom_call" | custom-call | tf_op jit(solution)/shard_map/swap_8/pallas_call | solution.py:175
  269.7 2.3 z_transform.3.src
  272.0 10.7 %deal_9.1 = f32[16,8,256]{2,1,0:T(8,128)} custom-call(f32[16,8,256]{2,1,0:T(8,128)} %z_transform.3.src), custom_call_target="tpu_custom_call" | custom-call | tf_op jit(solution)/shard_map/deal_9/pallas_call | solution.py:257
  285.9 6.8 %weight_grad.1 = f32[8,32,64,128]{3,2,1,0:T(8,128)} custom-call(bf16[32,16,64]{2,1,0:T(8,128)(2,1)} %bitcast.61, bf16[32,16,128]{2,1,0:T(8,128)(2,1)} %bitcast.60, bf16[16,1024]{1,0:T(8,128)(2,1)} %constant.39.clone.mask_ref), custom_call_target="tpu_custom_call" | custom-call | tf_op jit(solution)/shard_map/weight_grad/pallas_call | solution.py:481
  (65 shorter events, 15.8 us)
Async XLA Ops:
  44.8 79.8 %copy-start.5 = (f32[64]{0:T(128)S(1)}, f32[64]{0:T(128)}, u32[]{:S(2)}) copy-start(f32[64]{0:T(128)} %param.19) | copy-start | bytes 772
  44.8 80.5 %copy-start.3 = (bf16[64,64]{1,0:T(8,128)(2,1)S(1)}, bf16[64,64]{1,0:T(8,128)(2,1)}, u32[]{:S(2)}) copy-start(bf16[64,64]{1,0:T(8,128)(2,1)} %param.18) | copy-start | bytes 24580
  44.9 81.1 %copy-start.4 = (bf16[64,3]{0,1:T(4,128)(2,1)S(1)}, bf16[64,3]{0,1:T(4,128)(2,1)}, u32[]{:S(2)}) copy-start(bf16[64,3]{0,1:T(4,128)(2,1)} %param.20) | copy-start | bytes 1156
  189.4 31.9 %copy-start.2 = (f32[32,256]{1,0:T(8,128)S(1)}, f32[32,256]{1,0:T(8,128)}, u32[]{:S(2)}) copy-start(f32[32,256]{1,0:T(8,128)} %get-tuple-element.63) | copy-start | bytes 98308
  189.4 32.5 %copy-start.1 = (f32[3,16,256]{2,1,0:T(8,128)S(1)}, f32[3,16,256]{2,1,0:T(8,128)}, u32[]{:S(2)}) copy-start(f32[3,16,256]{2,1,0:T(8,128)} %get-tuple-element.64) | copy-start | bytes 147460
  269.7 22.9 %copy-start = (f32[8,40,128]{2,1,0:T(8,128)S(1)}, f32[8,40,128]{2,1,0:T(8,128)}, u32[]{:S(2)}) copy-start(f32[8,40,128]{2,1,0:T(8,128)} %get-tuple-element.70) | copy-start | bytes 491524

commit v2 on v1

--- a/solution.py
+++ b/solution.py
@@ -14,12 +14,12 @@
 C = 64
 GY, GZ = 16, 8
 LY, LZ = 16, 16
+YB = 2
 QZ = 4
 F32, BF16 = jnp.float32, jnp.bfloat16
 SCALE = math.sqrt(M * M * M / (NX * NY * NZ))
 CELLS = NX * NY * NZ
-TAIL_SCALE = 0.24
-TAIL = (0.08952144314768905, 0.15555677138787463, -0.15417797314110948, 0.6257953656595543, -0.6462531425989838, 0.5546601809863483, -0.12510264575439553)
+DENSITY = 1.0 / math.sqrt(math.pi)
 MESH = pl.DeviceIdType.MESH
 ANY = pl.BlockSpec(memory_space=pl.ANY)
 
@@ -40,7 +40,8 @@
     forward[16] = cos_x[:, 16]
     forward[17:32] = sin_x[:, 1:16].T
     forward[32] = sin_x[:, 16]
-    inverse = np.zeros((40, NX))
+    inverse = np.zeros((64, NX))
+    inverse[33:36] = 1.0
     inverse[0:32:2] = forward[:16]
     inverse[1:32:2] = forward[16:32]
     inverse[32] = forward[32]
@@ -99,14 +100,17 @@
             device_id={axis: peer}, device_id_type=MESH,
         )
 
-    copies, late = [], []
+    copies, early, late = [], [], []
     for index, mode in enumerate(modes):
         src, dst, send, recv = srcs[index], dsts[index], sends[index], recvs[index]
         if mode == "to0":
 
-            @pl.when(me != 0)
-            def _(src=src, dst=dst, send=send, recv=recv):
-                remote(src, dst.at[me], send.at[0], recv.at[me], 0).start()
+            def begin(step, src=src, dst=dst, send=send, recv=recv):
+                @pl.when(jnp.logical_and(me != 0, me == step))
+                def _():
+                    remote(src, dst.at[me], send.at[0], recv.at[me], 0).start()
+
+            early.append(begin)
 
             @pl.when(me == 0)
             def _(src=src, dst=dst, index=index):
@@ -146,14 +150,19 @@
             late.append(finish)
         else:
             piece = (lambda p, src=src: src.at[p]) if mode == "swap" else (lambda p, src=src: src)
-            copies.append(pltpu.make_async_copy(piece(me), dst.at[me], local.at[index]))
+            copies.append((0, pltpu.make_async_copy(piece(me), dst.at[me], local.at[index])))
             for step in range(1, count):
                 peer = (me + step) % count
                 copies.append(
-                    remote(piece(peer), dst.at[me], send.at[step], recv.at[step], peer)
+                    (step, remote(piece(peer), dst.at[me], send.at[step], recv.at[step], peer))
                 )
-    for copy in copies:
-        copy.start()
+    for step in range(count):
+        for at, copy in copies:
+            if at == step:
+                copy.start()
+        for begin in early:
+            begin(step)
+    copies = [copy for _, copy in copies]
     for copy in copies:
         copy.wait()
     for finish in late:
@@ -187,86 +196,6 @@
     return result if size > 1 else result[0]
 
 
-def deal_kernel(inward, src, dst, send, recv, local):
-    g, h = lax.axis_index("gy"), lax.axis_index("gz")
-    owners = [(2 * h + j % 2, j // 2) for j in range(GY)]
-    holders = [(k, g // 2) for k in range(GY)]
-    targets, sources = (holders, owners) if inward else (owners, holders)
-    slot = h * 2 + g % 2 if inward else g
-
-    def is_me(device):
-        return jnp.logical_and(device[0] == g, device[1] == h)
-
-    barrier = pltpu.get_barrier_semaphore()
-    for device in sources:
-
-        @pl.when(jnp.logical_not(is_me(device)))
-        def _(device=device):
-            pl.semaphore_signal(
-                barrier, inc=1, device_id={"gy": device[0], "gz": device[1]}, device_id_type=MESH
-            )
-
-    diagonal = g // 2 == h
-    pl.semaphore_wait(barrier, jnp.where(diagonal, GY - 1, GY))
-
-    def outgoing(j):
-        return pltpu.make_async_remote_copy(
-            src_ref=src.at[j],
-            dst_ref=dst.at[slot],
-            send_sem=send.at[j],
-            recv_sem=recv.at[slot],
-            device_id={"gy": targets[j][0], "gz": targets[j][1]},
-            device_id_type=MESH,
-        )
-
-    def incoming(j):
-        return pltpu.make_async_remote_copy(
-            src_ref=src.at[j],
-            dst_ref=dst.at[j],
-            send_sem=send.at[j],
-            recv_sem=recv.at[j],
-            device_id={"gy": sources[j][0], "gz": sources[j][1]},
-            device_id_type=MESH,
-        )
-
-    for j in range(GY):
-        mine = is_me(targets[j])
-
-        @pl.when(jnp.logical_not(mine))
-        def _(j=j):
-            outgoing(j).start()
-
-        @pl.when(mine)
-        def _(j=j):
-            copy = pltpu.make_async_copy(src.at[j], dst.at[slot], local.at[0])
-            copy.start()
-            copy.wait()
-
-    for j in range(GY):
-
-        @pl.when(jnp.logical_not(is_me(targets[j])))
-        def _(j=j):
-            outgoing(j).wait_send()
-
-        @pl.when(jnp.logical_not(is_me(sources[j])))
-        def _(j=j):
-            incoming(j).wait_recv()
-
-
-def deal(inward, collective_id, src):
-    return pl.pallas_call(
-        functools.partial(deal_kernel, inward),
-        out_shape=jax.ShapeDtypeStruct(src.shape, src.dtype),
-        in_specs=[ANY],
-        out_specs=ANY,
-        scratch_shapes=[pltpu.SemaphoreType.DMA((GY,))] * 2 + [pltpu.SemaphoreType.DMA((1,))],
-        compiler_params=pltpu.CompilerParams(
-            collective_id=collective_id, has_side_effects=True
-        ),
-        name=f"deal_{collective_id}",
-    )(src)
-
-
 def emit_rows(rows_ref, out_ref, extra_ref):
     for half in range(2):
         lanes = slice(half * 128, half * 128 + 128)
@@ -283,17 +212,22 @@
 
 
 def x_kernel(field_ref, table_ref, cells_ref, out_ref, extra_ref, stage, rows):
-    y = pl.program_id(0)
-    for half in range(2):
-        lanes = slice(half * 128, half * 128 + 128)
-        stage[half] = field_ref[:, 0, :, lanes].astype(F32).reshape(C * LZ, 128)
-        for z in range(LZ):
-            cells_ref[0, z, :, lanes] = stage[half, pl.ds(z, C, stride=LZ), :].astype(BF16)
-    for q in range(QZ):
-        block = cells_ref[0, q * 4 : q * 4 + 4].reshape(4 * C, NX)
-        put_rows(rows, y * QZ + q, dot(table_ref[...], block, NT))
-
-    @pl.when(y == LY - 1)
+    step = pl.program_id(0)
+
+    def plane(k, carry):
+        for half in range(2):
+            lanes = slice(half * 128, half * 128 + 128)
+            stage[half] = field_ref[:, k, :, lanes].astype(F32).reshape(C * LZ, 128)
+            for z in range(LZ):
+                cells_ref[k, z, :, lanes] = stage[half, pl.ds(z, C, stride=LZ), :].astype(BF16)
+        for q in range(QZ):
+            block = cells_ref[k, q * 4 : q * 4 + 4].reshape(4 * C, NX)
+            put_rows(rows, (step * YB + k) * QZ + q, dot(table_ref[...], block, NT))
+        return carry
+
+    lax.fori_loop(0, YB, plane, 0)
+
+    @pl.when(step == LY // YB - 1)
     def _():
         emit_rows(rows, out_ref, extra_ref)
 
@@ -302,13 +236,13 @@
     forward = const(tables()[0])
     return pl.pallas_call(
         x_kernel,
-        grid=(LY,),
+        grid=(LY // YB,),
         in_specs=[
-            pl.BlockSpec((C, 1, LZ, NX), lambda y: (0, y, 0, 0)),
+            pl.BlockSpec((C, YB, LZ, NX), lambda y: (0, y, 0, 0)),
             whole((40, NX)),
         ],
         out_specs=[
-            pl.BlockSpec((1, LZ, C, NX), lambda y: (y, 0, 0, 0)),
+            pl.BlockSpec((YB, LZ, C, NX), lambda y: (y, 0, 0, 0)),
             whole((GY, 2, 64, NX)),
             whole((64, NX)),
         ],
@@ -323,8 +257,7 @@
     )(field_in, forward)
 
 
-def y_kernel(first_ref, src_ref, extra_ref, table_ref, out_ref):
-    first = first_ref[0] == 0
+def y_body(first, src_ref, extra_ref, table_ref, out_ref):
     sums = []
     for part in range(2):
         sums.append(dot(table_ref[...], src_ref[:, part].reshape(GY * 64, NX)))
@@ -341,24 +274,7 @@
         out_ref[:, index] = part.astype(BF16).reshape(GZ, 16, NX)
 
 
-def y_transform(first, rows, extra):
-    return pl.pallas_call(
-        y_kernel,
-        in_specs=[
-            pl.BlockSpec(memory_space=pltpu.SMEM),
-            pl.BlockSpec(memory_space=pltpu.VMEM),
-            pl.BlockSpec(memory_space=pltpu.VMEM),
-            pl.BlockSpec(memory_space=pltpu.VMEM),
-        ],
-        out_specs=pl.BlockSpec(memory_space=pltpu.VMEM),
-        out_shape=jax.ShapeDtypeStruct((GZ, 4, 16, NX), BF16),
-        compiler_params=params(),
-        name="y_transform",
-    )(first, rows, extra, const(tables()[2]))
-
-
-def y_back_kernel(first_ref, src_ref, table_ref, out_ref, extra_ref):
-    first = first_ref[0] == 0
+def y_back_body(first, src_ref, table_ref, out_ref, extra_ref):
     ar, ai, br, bi = [
         src_ref[:, part].reshape(128, NX).astype(F32) for part in range(4)
     ]
@@ -376,25 +292,7 @@
             extra_ref[...] = result
 
 
-def y_back(first, modes):
-    return pl.pallas_call(
-        y_back_kernel,
-        in_specs=[
-            pl.BlockSpec(memory_space=pltpu.SMEM),
-            pl.BlockSpec(memory_space=pltpu.VMEM),
-            pl.BlockSpec(memory_space=pltpu.VMEM),
-        ],
-        out_specs=[pl.BlockSpec(memory_space=pltpu.VMEM)] * 2,
-        out_shape=[
-            jax.ShapeDtypeStruct((GY, 2, 64, NX), BF16),
-            jax.ShapeDtypeStruct((GY, 64, NX), BF16),
-        ],
-        compiler_params=params(),
-        name="y_back",
-    )(first, modes, const(tables()[2].T))
-
-
-def z_kernel(factor, src_ref, table_ref, out_ref):
+def z_body(factor, src_ref, table_ref, out_ref):
     for m in range(2):
         sums = []
         for p in range(2):
@@ -414,18 +312,7 @@
         ).reshape(GY, 8, 128)
 
 
-def z_transform(modes, factor):
-    return pl.pallas_call(
-        functools.partial(z_kernel, factor),
-        in_specs=[pl.BlockSpec(memory_space=pltpu.VMEM)] * 2,
-        out_specs=pl.BlockSpec(memory_space=pltpu.VMEM),
-        out_shape=jax.ShapeDtypeStruct((GY, 8, 256), F32),
-        compiler_params=params(),
-        name="z_transform",
-    )(modes, const(tables()[3]))
-
-
-def z_back_kernel(src_ref, table_ref, out_ref):
+def z_back_body(src_ref, table_ref, out_ref):
     for m in range(2):
         block = src_ref[:, :, m * 128 : m * 128 + 128].reshape(128, 128).astype(BF16)
         real, imag = [], []
@@ -439,15 +326,184 @@
             out_ref[:, m * 2 + p] = full.reshape(GZ, 16, NX)
 
 
-def z_back(modes):
+def mode_places():
+    g, h = lax.axis_index("gy"), lax.axis_index("gz")
+    owners = [(2 * h + j % 2, j // 2) for j in range(GY)]
+    holders = [(k, g // 2) for k in range(GY)]
+    return g, h, owners, holders
+
+
+def greet(g, h, sources, with_gy):
+    barrier = pltpu.get_barrier_semaphore()
+    for step in range(1, GZ):
+        pl.semaphore_signal(
+            barrier, inc=1, device_id={"gz": (h + step) % GZ}, device_id_type=MESH
+        )
+    if with_gy:
+        for step in range(1, GY):
+            pl.semaphore_signal(
+                barrier, inc=1, device_id={"gy": (g + step) % GY}, device_id_type=MESH
+            )
+    for y, z in sources:
+
+        @pl.when(jnp.logical_not(jnp.logical_and(y == g, z == h)))
+        def _(y=y, z=z):
+            pl.semaphore_signal(barrier, inc=1, device_id={"gy": y, "gz": z}, device_id_type=MESH)
+
+
+def await_greetings(g, h, with_gy):
+    fixed = GZ - 1 + (GY - 1 if with_gy else 0)
+    pl.semaphore_wait(
+        pltpu.get_barrier_semaphore(), jnp.where(g // 2 == h, GY - 1, GY) + fixed
+    )
+
+
+def spread(axis, count, me, piece, dst, send, recv, local):
+    copies = [pltpu.make_async_copy(piece(me), dst.at[me], local)]
+    for step in range(1, count):
+        peer = (me + step) % count
+        copies.append(
+            pltpu.make_async_remote_copy(
+                src_ref=piece(peer), dst_ref=dst.at[me],
+                send_sem=send.at[step], recv_sem=recv.at[step],
+                device_id={axis: peer}, device_id_type=MESH,
+            )
+        )
+    for copy in copies:
+        copy.start()
+    return copies
+
+
+def deal(g, h, targets, sources, slot, src, dst, send, recv, local):
+    def is_me(device):
+        return jnp.logical_and(device[0] == g, device[1] == h)
+
+    def remote(j, device, landing, arrived):
+        return pltpu.make_async_remote_copy(
+            src_ref=src.at[j], dst_ref=dst.at[landing],
+            send_sem=send.at[j], recv_sem=recv.at[arrived],
+            device_id={"gy": device[0], "gz": device[1]}, device_id_type=MESH,
+        )
+
+    for j in range(GY):
+        mine = is_me(targets[j])
+
+        @pl.when(jnp.logical_not(mine))
+        def _(j=j):
+            remote(j, targets[j], slot, slot).start()
+
+        @pl.when(mine)
+        def _(j=j):
+            copy = pltpu.make_async_copy(src.at[j], dst.at[slot], local)
+            copy.start()
+            copy.wait()
+
+    for j in range(GY):
+
+        @pl.when(jnp.logical_not(is_me(targets[j])))
+        def _(j=j):
+            remote(j, targets[j], slot, slot).wait_send()
+
+        @pl.when(jnp.logical_not(is_me(sources[j])))
+        def _(j=j):
+            remote(j, sources[j], j, j).wait_recv()
+
+
+def to_modes_kernel(factor, with_small, *refs):
+    if with_small:
+        (rows, extra, y_table, z_table, small, dealt, small_out, y_out, z_in, z_out,
+         send, recv, send2, recv2, local, small_a, small_b, small_c,
+         send3, recv3, send4, recv4) = refs
+    else:
+        (rows, extra, y_table, z_table, dealt, y_out, z_in, z_out,
+         send, recv, send2, recv2, local) = refs
+    g, h, owners, holders = mode_places()
+    greet(g, h, holders, with_small)
+    y_body(g == 0, rows, extra, y_table, y_out)
+    if with_small:
+        small_a[...] = jnp.sum(small[...], axis=0)
+    await_greetings(g, h, with_small)
+    copies = spread("gz", GZ, h, lambda p: y_out.at[p], z_in, send, recv, local.at[0])
+    if with_small:
+        copies += spread("gz", GZ, h, lambda p: small_a, small_b, send3, recv3, local.at[1])
+    for copy in copies:
+        copy.wait()
+    z_body(factor, z_in, z_table, z_out)
+    copies = []
+    if with_small:
+        small_c[...] = jnp.sum(small_b[...], axis=0)
+        copies = spread("gy", GY, g, lambda p: small_c, small_out, send4, recv4, local.at[2])
+    deal(g, h, owners, holders, g, z_out, dealt, send2, recv2, local.at[3])
+    for copy in copies:
+        copy.wait()
+
+
+def to_modes(collective_id, factor, rows, extra, small=None):
+    vmem = pl.BlockSpec(memory_space=pltpu.VMEM)
+    args = [rows, extra, const(tables()[2]), const(tables()[3])]
+    outs = [jax.ShapeDtypeStruct((GY, 8, 256), F32)]
+    block = pltpu.VMEM((GZ, 4, 16, NX), BF16)
+    gz_sems = [pltpu.SemaphoreType.DMA((GZ,))] * 2
+    gy_sems = [pltpu.SemaphoreType.DMA((GY,))] * 2
+    scratch = [block, block, pltpu.VMEM((GY, 8, 256), F32)]
+    scratch += gz_sems + gy_sems + [pltpu.SemaphoreType.DMA((4,))]
+    if small is not None:
+        args.append(small)
+        outs.append(jax.ShapeDtypeStruct((GY, 8, 128), F32))
+        scratch += [
+            pltpu.VMEM((8, 128), F32),
+            pltpu.VMEM((GZ, 8, 128), F32),
+            pltpu.VMEM((8, 128), F32),
+        ]
+        scratch += gz_sems + gy_sems
+    result = pl.pallas_call(
+        functools.partial(to_modes_kernel, factor, small is not None),
+        out_shape=outs,
+        in_specs=[vmem] * len(args),
+        out_specs=[ANY] * len(outs),
+        scratch_shapes=scratch,
+        compiler_params=pltpu.CompilerParams(
+            collective_id=collective_id, has_side_effects=True, vmem_limit_bytes=40 << 20
+        ),
+        name=f"to_modes_{collective_id}",
+    )(*args)
+    return result if small is not None else result[0]
+
+
+def from_modes_kernel(
+    modes, y_table, z_table, rows, extra, landed, z_out, y_in, send, recv, send2, recv2, local
+):
+    g, h, owners, holders = mode_places()
+    greet(g, h, owners, False)
+    await_greetings(g, h, False)
+    deal(g, h, holders, owners, h * 2 + g % 2, modes, landed, send2, recv2, local.at[1])
+    z_back_body(landed, z_table, z_out)
+    copies = spread("gz", GZ, h, lambda p: z_out.at[p], y_in, send, recv, local.at[0])
+    for copy in copies:
+        copy.wait()
+    y_back_body(g == 0, y_in, y_table, rows, extra)
+
+
+def from_modes(collective_id, modes):
+    vmem = pl.BlockSpec(memory_space=pltpu.VMEM)
+    block = pltpu.VMEM((GZ, 4, 16, NX), BF16)
     return pl.pallas_call(
-        z_back_kernel,
-        in_specs=[pl.BlockSpec(memory_space=pltpu.VMEM)] * 2,
-        out_specs=pl.BlockSpec(memory_space=pltpu.VMEM),
-        out_shape=jax.ShapeDtypeStruct((GZ, 4, 16, NX), BF16),
-        compiler_params=params(),
-        name="z_back",
-    )(modes, const(tables()[3].transpose(0, 1, 3, 2)))
+        from_modes_kernel,
+        out_shape=[
+            jax.ShapeDtypeStruct((GY, 2, 64, NX), BF16),
+            jax.ShapeDtypeStruct((GY, 64, NX), BF16),
+        ],
+        in_specs=[vmem] * 3,
+        out_specs=[vmem] * 2,
+        scratch_shapes=[pltpu.VMEM((GY, 8, 256), F32), block, block]
+        + [pltpu.SemaphoreType.DMA((GZ,))] * 2
+        + [pltpu.SemaphoreType.DMA((GY,))] * 2
+        + [pltpu.SemaphoreType.DMA((2,))],
+        compiler_params=pltpu.CompilerParams(
+            collective_id=collective_id, has_side_effects=True, vmem_limit_bytes=40 << 20
+        ),
+        name=f"from_modes_{collective_id}",
+    )(modes, const(tables()[2].T), const(tables()[3].transpose(0, 1, 3, 2)))
 
 
 def to_kx(dealt):
@@ -493,24 +549,13 @@
     )(u, g, mask)
 
 
-def normal_parts(value):
-    size = jnp.abs(value)
-    decay = jnp.exp(-0.5 * value * value)
-    t = 1.0 / (1.0 + TAIL_SCALE * size)
-    poly = jnp.full_like(value, TAIL[-1])
-    for coefficient in TAIL[-2::-1]:
-        poly = poly * t + coefficient
-    tail = poly * t * decay
-    return jnp.where(value < 0.0, tail, 1.0 - tail), decay * (1.0 / math.sqrt(2.0 * math.pi))
-
-
 def dense_kernel(
     rows_ref, odd_ref, cells_ref, table_ref, point_ref, bias_ref, out_w_ref, out_b_ref,
     hidden_ref, slope_ref, field_ref, low_ref, high_ref, corner_ref, rows,
 ):
-    y = pl.program_id(0)
-
-    @pl.when(y == 0)
+    step = pl.program_id(0)
+
+    @pl.when(step == 0)
     def _():
         corner_ref[...] = jnp.zeros_like(corner_ref)
         for half in range(2):
@@ -518,66 +563,80 @@
             for g in range(GY * 2):
                 rows[half, g * 64 : g * 64 + 64, :] = rows_ref[g, :, lanes].astype(F32)
             rows[half, 2048:2112, :] = odd_ref[:, lanes].astype(F32)
-            rows[half, 2112:2560, :] = jnp.zeros((448, 128), F32)
-
-    def quad(q, carry):
-        picked = jnp.concatenate(
-            [rows[half, pl.ds(y * QZ + q, 40, stride=64), :] for half in range(2)], axis=1
-        ).astype(BF16)
-        spectral = dot(picked, table_ref[...], TN)
-        for inner in range(4):
-            z = q * 4 + inner
-            pre = (
-                spectral[inner * C : inner * C + C]
-                + dot(point_ref[...], cells_ref[0, z])
-                + bias_ref[...]
+            rest = bias_ref[...]
+            for part in range(3):
+                piece = rest.astype(BF16).astype(F32)
+                start = 2112 + part * 64
+                rows[half, start : start + 64, :] = jnp.broadcast_to(piece, (64, 128))
+                rest = rest - piece
+            rows[half, 2304:3072, :] = jnp.zeros((768, 128), F32)
+
+    def plane(k, carry):
+        y = step * YB + k
+        for q in range(QZ):
+            picked = jnp.concatenate(
+                [rows[half, pl.ds(y * QZ + q, 48, stride=64), :] for half in range(2)], axis=1
             )
-            normal_cdf, density = normal_parts(pre)
-            hidden = (pre * normal_cdf).astype(BF16)
-            hidden_ref[0, z] = hidden
-            slope_ref[0, z] = (normal_cdf + pre * density).astype(BF16)
-            b_rows = dot(out_w_ref[...], hidden)
-            for b in range(3):
-                field_ref[b, 0, pl.ds(z, 1), :] = b_rows[b : b + 1] + out_b_ref[b]
+            picked = jnp.concatenate(
+                [jnp.zeros((64, NX), F32), picked, jnp.zeros((16, NX), F32)], axis=0
+            )
+            left = picked.T.astype(BF16)
+            for inner in range(4):
+                z = q * 4 + inner
+                pre = dot(
+                    left[inner * C : inner * C + C] + point_ref[...],
+                    jnp.concatenate([cells_ref[k, z], table_ref[...]], axis=0),
+                )
+                scaled = pre * math.sqrt(0.5)
+                normal_cdf = 0.5 * lax.erf(scaled) + 0.5
+                decay = jnp.exp2(scaled * scaled * -math.log2(math.e))
+                hidden = (pre * normal_cdf).astype(BF16)
+                hidden_ref[k, z] = hidden
+                slope_ref[k, z] = (normal_cdf + scaled * DENSITY * decay).astype(BF16)
+                b_rows = dot(out_w_ref[...], hidden)
+                for b in range(3):
+                    field_ref[b, k, z : z + 1, :] = b_rows[b : b + 1] + out_b_ref[b]
+        for b in range(3):
+            for i in range(2):
+                z = LZ - 2 + i
+                low_ref[b, pl.ds(y * 2 + i, 1), :] = field_ref[b, k, i : i + 1, :]
+                high_ref[b, pl.ds(y * 2 + i, 1), :] = field_ref[b, k, z : z + 1, :]
         return carry
 
-    lax.fori_loop(0, QZ, quad, 0)
-    for b in range(3):
-        for i in range(2):
-            z = LZ - 2 + i
-            low_ref[b, pl.ds(y * 2 + i, 1), :] = field_ref[b, 0, i : i + 1, :]
-            high_ref[b, pl.ds(y * 2 + i, 1), :] = field_ref[b, 0, z : z + 1, :]
+    lax.fori_loop(0, YB, plane, 0)
     for y_edge in range(2):
 
-        @pl.when(y == y_edge * (LY - 1))
+        @pl.when(step == y_edge * (LY // YB - 1))
         def _(y_edge=y_edge):
             for b in range(3):
                 for z_edge in range(2):
                     z = z_edge * (LZ - 1)
-                    corner_ref[y_edge * 2 + z_edge, b : b + 1, :] = field_ref[b, 0, z : z + 1, :]
+                    corner_ref[y_edge * 2 + z_edge, b : b + 1, :] = field_ref[
+                        b, y_edge * (YB - 1), z : z + 1, :
+                    ]
 
 
 def dense(rows, odd, cells, point_weight, point_bias, out_weight, out_bias):
     out_w = jnp.pad(out_weight.T, ((0, 5), (0, 0)))
-    cell_spec = pl.BlockSpec((1, LZ, C, NX), lambda y: (y, 0, 0, 0))
+    cell_spec = pl.BlockSpec((YB, LZ, C, NX), lambda y: (y, 0, 0, 0))
     cell_shape = jax.ShapeDtypeStruct((LY, LZ, C, NX), BF16)
     return pl.pallas_call(
         dense_kernel,
-        grid=(LY,),
+        grid=(LY // YB,),
         in_specs=[
             whole((GY * 2, 64, NX)),
             whole((64, NX)),
             cell_spec,
-            whole((40, NX)),
-            whole((C, C)),
-            whole((C, 1)),
+            whole((64, NX)),
+            whole((C, 128)),
+            whole((1, 128)),
             whole((8, C)),
             pl.BlockSpec(memory_space=pltpu.SMEM),
         ],
         out_specs=[
             cell_spec,
             cell_spec,
-            pl.BlockSpec((3, 1, LZ, NX), lambda y: (0, y, 0, 0)),
+            pl.BlockSpec((3, YB, LZ, NX), lambda y: (0, y, 0, 0)),
             whole((3, 32, NX)),
             whole((3, 32, NX)),
             whole((4, 8, NX)),
@@ -590,7 +649,7 @@
             jax.ShapeDtypeStruct((3, 32, NX), F32),
             jax.ShapeDtypeStruct((4, 8, NX), F32),
         ],
-        scratch_shapes=[pltpu.VMEM((2, 40 * 64, 128), F32)],
+        scratch_shapes=[pltpu.VMEM((2, 48 * 64, 128), F32)],
         compiler_params=params(),
         name="dense",
     )(
@@ -598,52 +657,58 @@
         odd,
         cells,
         const(tables()[1]),
-        point_weight.T,
-        point_bias[:, None],
+        jnp.pad(point_weight.T, ((0, 0), (0, C))),
+        jnp.concatenate([point_bias, point_bias])[None],
         out_w,
         out_bias,
     )
 
 
 def grad_kernel(
-    hidden_ref, slope_ref, cells_ref, grad_ref, table_ref, out_w_ref,
-    rows_ref, odd_ref, point_ref, bias_ref, out_ref,
+    hidden_ref, slope_ref, cells_ref, grad_ref, table_ref, out_w_ref, loss_ref,
+    rows_ref, odd_ref, small_ref,
     stage, rows, point_sum, bias_sum, out_sum,
 ):
-    y = pl.program_id(0)
-
-    @pl.when(y == 0)
+    step = pl.program_id(0)
+
+    @pl.when(step == 0)
     def _():
         point_sum[...] = jnp.zeros_like(point_sum)
         bias_sum[...] = jnp.zeros_like(bias_sum)
         out_sum[...] = jnp.zeros_like(out_sum)
 
-    def quad(q, carry):
-        for inner in range(4):
-            z = q * 4 + inner
-            grad = jnp.concatenate(
-                [grad_ref[b, 0, pl.ds(z, 1), :] for b in range(3)] + [jnp.zeros((5, NX), F32)],
-                axis=0,
-            )
-            upper = grad.astype(BF16)
-            lower = (grad - upper.astype(F32)).astype(BF16)
-            both = jnp.concatenate([upper, lower], axis=0)
-            grad_hidden = dot(out_w_ref[...], both)
-            stage[inner * C : inner * C + C, :] = (
-                grad_hidden * slope_ref[0, z].astype(F32)
-            ).astype(BF16)
-            out_sum[...] += dot(both, hidden_ref[0, z], NT)
-        block = stage[...]
-        x_rows = dot(table_ref[...], block, NT)
-        put_rows(rows, y * QZ + q, x_rows)
-        bias_sum[...] += x_rows[0:8]
-        cells = cells_ref[0, pl.ds(q * 4, 4)].reshape(4 * C, NX)
-        point_sum[...] += dot(cells, block, NT)
+    def plane(k, carry):
+        out_total, bias_total = None, None
+        for q in range(QZ):
+            for inner in range(4):
+                z = q * 4 + inner
+                grad = jnp.concatenate(
+                    [grad_ref[b, k, z : z + 1, :] for b in range(3)] + [jnp.zeros((5, NX), F32)],
+                    axis=0,
+                )
+                upper = grad.astype(BF16)
+                lower = (grad - upper.astype(F32)).astype(BF16)
+                both = jnp.concatenate([upper, lower], axis=0)
+                grad_hidden = dot(out_w_ref[...], both)
+                stage[inner * C : inner * C + C, q * NX : q * NX + NX] = (
+                    grad_hidden * slope_ref[k, z].astype(F32)
+                ).astype(BF16)
+                out_term = dot(both, hidden_ref[k, z], NT)
+                out_total = out_term if out_total is None else out_total + out_term
+            x_rows = dot(table_ref[...], stage[:, q * NX : q * NX + NX], NT)
+            put_rows(rows, (step * YB + k) * QZ + q, x_rows)
+            bias_total = x_rows[0:8] if bias_total is None else bias_total + x_rows[0:8]
+        out_sum[...] += out_total
+        bias_sum[...] += bias_total
+        cells = jnp.concatenate(
+            [cells_ref[k, q * 4 : q * 4 + 4].reshape(4 * C, NX) for q in range(QZ)], axis=1
+        )
+        point_sum[...] += dot(cells, stage[...], NT)
         return carry
 
-    lax.fori_loop(0, QZ, quad, 0)
-
-    @pl.when(y == LY - 1)
+    lax.fori_loop(0, YB, plane, 0)
+
+    @pl.when(step == LY // YB - 1)
     def _():
         emit_rows(rows, rows_ref, odd_ref)
         total = point_sum[0:C, 0:C]
@@ -652,43 +717,42 @@
             span = slice(inner * C, inner * C + C)
             total = total + point_sum[span, span]
             bias = bias + bias_sum[0:1, span]
-        point_ref[...] = total
-        bias_ref[...] = bias
-        out_ref[...] = out_sum[0:8] + out_sum[8:16]
-
-
-def grad_dense(hidden, slope, cells, grad_b, out_weight):
+        small_ref[...] = jnp.zeros_like(small_ref)
+        small_ref[0:C, 0:C] = total
+        small_ref[64:65, 0:C] = bias
+        small_ref[72:80, 0:C] = out_sum[0:8] + out_sum[8:16]
+        small_ref[80:88, :] = loss_ref[:, 0:128] + loss_ref[:, 128:256]
+
+
+def grad_dense(hidden, slope, cells, grad_b, out_weight, loss_rows):
     forward = const(tables()[0])
     out_w = jnp.pad(out_weight, ((0, 0), (0, 5)))
     out_w = jnp.concatenate([out_w, out_w], axis=1)
-    cell_spec = pl.BlockSpec((1, LZ, C, NX), lambda y: (y, 0, 0, 0))
+    cell_spec = pl.BlockSpec((YB, LZ, C, NX), lambda y: (y, 0, 0, 0))
     return pl.pallas_call(
         grad_kernel,
-        grid=(LY,),
+        grid=(LY // YB,),
         in_specs=[
             cell_spec,
             cell_spec,
             cell_spec,
-            pl.BlockSpec((3, 1, LZ, NX), lambda y: (0, y, 0, 0)),
+            pl.BlockSpec((3, YB, LZ, NX), lambda y: (0, y, 0, 0)),
             whole((40, NX)),
             whole((C, 16)),
+            whole((8, NX)),
         ],
         out_specs=[
             whole((GY, 2, 64, NX)),
             whole((64, NX)),
-            whole((C, C)),
-            whole((1, C)),
-            whole((8, C)),
+            whole((128, 128)),
         ],
         out_shape=[
             jax.ShapeDtypeStruct((GY, 2, 64, NX), BF16),
             jax.ShapeDtypeStruct((64, NX), BF16),
-            jax.ShapeDtypeStruct((C, C), F32),
-            jax.ShapeDtypeStruct((1, C), F32),
-            jax.ShapeDtypeStruct((8, C), F32),
+            jax.ShapeDtypeStruct((128, 128), F32),
         ],
         scratch_shapes=[
-            pltpu.VMEM((4 * C, NX), BF16),
+            pltpu.VMEM((4 * C, QZ * NX), BF16),
             pltpu.VMEM((2, 40 * 64, 128), F32),
             pltpu.VMEM((4 * C, 4 * C), F32),
             pltpu.VMEM((8, NX), F32),
@@ -696,7 +760,7 @@
         ],
         compiler_params=params(),
         name="grad_dense",
-    )(hidden, slope, cells, grad_b, forward, out_w)
+    )(hidden, slope, cells, grad_b, forward, out_w, loss_rows)
 
 
 DIRECTIONS = [(dy, dz) for dy in (-1, 0, 1) for dz in (-1, 0, 1) if dy or dz]
@@ -790,7 +854,7 @@
 
 def stencil_kernel(
     place_ref, field_ref, y_low_ref, y_high_ref, z_low_ref, z_high_ref, corner_ref,
-    grad_ref, loss_ref, bias_ref, wide, own, slopes,
+    grad_ref, loss_ref, wide, own, slopes,
 ):
     g, h = place_ref[0], place_ref[1]
     zero_rows = jnp.zeros((8, NX), F32)
@@ -847,7 +911,7 @@
         return loss + jnp.where(jnp.logical_and(inner, counted), terms, 0.0)
 
     loss = lax.fori_loop(1, 19, one, jnp.zeros((32, NX), F32))
-    loss_ref[...] = loss
+    total_loss = loss
 
     def finish(y, sums):
         result = []
@@ -860,8 +924,9 @@
         return tuple(result)
 
     sums = lax.fori_loop(0, LY, finish, tuple(jnp.zeros((LZ, NX), F32) for _ in range(3)))
-    for b in range(3):
-        bias_ref[b] = sums[b]
+    loss_ref[...] = jnp.zeros_like(loss_ref)
+    for index, value in enumerate((total_loss,) + sums):
+        loss_ref[index : index + 1, :] = jnp.sum(value, axis=0, keepdims=True)
 
 
 def stencil(place, field, *halos):
@@ -869,11 +934,10 @@
     return pl.pallas_call(
         stencil_kernel,
         in_specs=[pl.BlockSpec(memory_space=pltpu.SMEM)] + [vmem] * 6,
-        out_specs=[vmem] * 3,
+        out_specs=[vmem] * 2,
         out_shape=[
             jax.ShapeDtypeStruct((3, LY, LZ, NX), F32),
-            jax.ShapeDtypeStruct((32, NX), F32),
-            jax.ShapeDtypeStruct((3, LZ, NX), F32),
+            jax.ShapeDtypeStruct((8, NX), F32),
         ],
         scratch_shapes=[
             pltpu.VMEM((3, 20, 32, NX), F32),
@@ -886,12 +950,10 @@
 
 
 def on_device(field_in, spectral_weight, point_weight, point_bias, out_weight, out_bias):
-    first = lax.axis_index("gy").astype(jnp.int32).reshape(1)
     place = jnp.stack([lax.axis_index("gy"), lax.axis_index("gz")]).astype(jnp.int32)
     cells, rows, odd = x_transform(field_in)
     rows, odd = swap("gy", GY, 1, ("swap", rows), ("to0", odd))
-    modes = swap("gz", GZ, 2, ("swap", y_transform(first, rows, odd)))
-    modes_in = to_kx(deal(False, 3, z_transform(modes, SCALE)).astype(BF16))
+    modes_in = to_kx(to_modes(2, SCALE, rows, odd).astype(BF16))
 
     mixed = jnp.einsum(
         "abkpi,abkio->abkpo", modes_in, spectral_weight, preferred_element_type=F32
@@ -900,44 +962,28 @@
     imag = mixed[..., 0, C:] + mixed[..., 1, :C]
     modes_out = jnp.stack([real, imag], axis=3)
 
-    back = z_back(deal(True, 4, from_kx(modes_out)))
-    rows, odd = y_back(first, swap("gz", GZ, 5, ("swap", back)))
+    rows, odd = from_modes(4, from_kx(modes_out))
     rows, odd = swap("gy", GY, 6, ("swap", rows), ("from0", odd))
 
     hidden, slope, field_b, *edges = dense(
         rows, odd, cells, point_weight, point_bias, out_weight, out_bias
     )
-    grad_b, loss_rows, bias_rows = stencil(place, field_b, *halo(10, field_b, *edges))
-    rows, odd, point_part, point_bias_part, out_part = grad_dense(
-        hidden, slope, cells, grad_b, out_weight
-    )
-    small = jnp.concatenate(
-        [
-            jnp.sum(loss_rows).reshape(1),
-            jnp.sum(bias_rows, axis=(1, 2)),
-            point_bias_part[0],
-            out_part[:3].reshape(-1),
-        ]
-    )
-    small = jnp.concatenate(
-        [point_part.reshape(32, 128), jnp.pad(small, (0, 1024 - 260)).reshape(8, 128)]
-    )
-    rows, odd, small = swap("gy", GY, 7, ("swap", rows), ("to0", odd), ("all", small))
-    modes, small = swap(
-        "gz", GZ, 8, ("swap", y_transform(first, rows, odd)), ("all", jnp.sum(small, axis=0))
-    )
-    small = jnp.sum(small, axis=0)
-    grad_modes = to_kx(deal(False, 9, z_transform(modes, 1.0)).astype(BF16))
+    grad_b, loss_rows = stencil(place, field_b, *halo(10, field_b, *edges))
+    rows, odd, small = grad_dense(hidden, slope, cells, grad_b, out_weight, loss_rows)
+    small = small.reshape(GY, 8, 128)
+    rows, odd, small = swap("gy", GY, 7, ("swap", rows), ("to0", odd), ("swap", small))
+    dealt, small = to_modes(8, 1.0, rows, odd, small)
+    small = small.reshape(128, 128)
+    grad_modes = to_kx(dealt.astype(BF16))
     grad_spectral = weight_grad(modes_in, grad_modes).reshape(4, 2, M, C, 2 * C)
-    grad_point = small[:32].reshape(C, C)
-    rest = small[32:].reshape(-1)
+    scalars = jnp.sum(small[80:84], axis=1)
     return (
-        rest[0] / CELLS,
+        scalars[0] / CELLS,
         grad_spectral,
-        grad_point,
-        rest[4:68],
-        rest[68:260].reshape(3, C).T,
-        rest[1:4],
+        small[:C, :C],
+        small[64, :C],
+        small[72:75, :C].T,
+        scalars[1:4],
     )
 
 

time: 299 us -> 243 us (0.81)
  Pallas kernels: 273 us -> 220 us
  other arithmetic: 8.93 us -> 3.49 us
  local copies, waits for them, and re-layouts: 9.89 us -> 13.3 us
    pallas_call x6 -> x3, Pallas kernels: 109 us -> 71.5 us  [swap(): pl.pallas_call(functools.partial(swap_kernel, axis, count, modes), out_sh...]
    pallas_call x12 -> x6, Pallas kernels: 141 us -> 127 us  [the longest x2 33.9 us: to_modes(): pl.pallas_call(functools.partial(to_modes_kernel, factor, small is not No...]
    unnamed x15 -> x31, local copies, waits for them, and re-layouts: 0.76 us -> 7.33 us
where the time goes in v2:
time: 243 us; the launch traced here: 242 us
  Pallas kernels  220 us (91%)
  local copies, waits for them, and re-layouts  13.3 us (5%)
  other arithmetic  3.49 us (1%)
  matrix products  3.37 us (1%)
    pallas_call x3, Pallas kernels, swap(): pl.pallas_call(functools.partial(swap_kernel, axis, count, modes), out_sh...  71.5 us
    pallas_call x2, Pallas kernels, to_modes(): pl.pallas_call(functools.partial(to_modes_kernel, factor, small is not No...  33.9 us
    pallas_call x1, Pallas kernels, dense(): pl.pallas_call(dense_kernel, grid=(LY // YB,), in_specs=[whole((GY * 2, 6...  33 us
    pallas_call x1, Pallas kernels, from_modes(): pl.pallas_call(from_modes_kernel, out_shape=[jax.ShapeDtypeStruct((GY, 2,...  24.1 us
    pallas_call x1, Pallas kernels, grad_dense(): pl.pallas_call(grad_kernel, grid=(LY // YB,), in_specs=[cell_spec, cell_s...  20.3 us
    pallas_call x1, Pallas kernels, x_transform(): pl.pallas_call(x_kernel, grid=(LY // YB,), in_specs=[pl.BlockSpec((C, YB,...  15.2 us
    pallas_call x1, Pallas kernels, halo(): pl.pallas_call(halo_kernel, out_shape=[side, side, edge, edge, jax.ShapeD...  7.44 us
    unnamed x31, local copies, waits for them, and re-layouts  7.33 us

profile of v2, /device:TPU:1, one launch (start us, length us, event | category | flops | bytes accessed | tf_op | source)
XLA Modules:
  0.0 242.0 jit_solution(15240650113149897096)
XLA Ops:
  0.7 15.2 %x_transform.1 = (bf16[16,16,64,256]{3,2,1,0:T(8,128)(2,1)}, bf16[16,2,64,256]{3,2,1,0:T(8,128)(2,1)}, bf16[64,256]{1,0:T(8,128)(2,1)}) custom-call(bf16[64,16,16,256]{3,2,1,0:T(8,128)(2,1)} %field_ref.1, bf16[40,256]{1,0:T(8,128)(2,1)} %constant.32.clone.table_ref), custom_call_target="tpu_custom_call" | custom-call | tf_op jit(solution)/shard_map/x_transform/pallas_call | solution.py:237
  15.9 24.1 %swap_1.1 = (bf16[16,2,64,256]{3,2,1,0:T(8,128)(2,1)}, bf16[16,64,256]{2,1,0:T(8,128)(2,1)}) custom-call(bf16[16,2,64,256]{3,2,1,0:T(8,128)(2,1)} %get-tuple-element.36.refs_0_, bf16[64,256]{1,0:T(8,128)(2,1)} %get-tuple-element.37.refs_1_), custom_call_target="tpu_custom_call" | custom-call | tf_op jit(solution)/shard_map/swap_1/pallas_call | solution.py:184
  40.1 1.2 copy-done.4
  41.3 1.0 copy-done.7
  42.3 17.2 %to_modes_2.1 = f32[16,8,256]{2,1,0:T(8,128)S(1)} custom-call(bf16[16,2,64,256]{3,2,1,0:T(8,128)(2,1)S(1)} %copy-done.4, bf16[16,64,256]{2,1,0:T(8,128)(2,1)S(1)} %copy-done.7, bf16[256,1024]{1,0:T(8,128)(2,1)S(1)} %copy-done, bf16[2,4,128,128]{3,2,1,0:T(8,128)(2,1)S(1)} %copy-done.1), custom_call_target="tpu_custom_call" | custom-call | tf_op jit(solution)/shard_map/to_modes_2/pallas_call | solution.py:459
  59.8 3.4 %fusion = f32[4,2,32,2,128]{4,3,2,1,0:T(2,128)S(1)} fusion(bf16[4,2,32,64,128]{4,3,2,1,0:T(8,128)(2,1)} %param.17, bf16[15,4,2,2,64]{4,3,0,2,1:T(2,128)(2,1)S(1)} %rev.9, bf16[1,4,2,2,64]{4,3,0,2,1:T(2,128)(2,1)S(1)} %slice_bitcast_fusion.4, bf16[16,4,2,2,64]{4,3,0,2,1:T(2,128)(2,1)S(1)} %copy_bitcast_fusion.2), kind=kOutput, calls=%fused_computation.9 | convolution fusion | flops 8585216 | bytes 4521984 | tf_op jit(solution)/shard_map/abkpi,abkio->abkpo/dot_general | solution.py:958
  63.2 0.6 slice_subtract_fusion
  64.9 24.1 %from_modes_4.1 = (bf16[16,2,64,256]{3,2,1,0:T(8,128)(2,1)S(1)}, bf16[16,64,256]{2,1,0:T(8,128)(2,1)S(1)}) custom-call(f32[16,8,256]{2,1,0:T(8,128)S(1)} %reshape.46.modes, bf16[1024,256]{1,0:T(8,128)(2,1)S(1)} %copy-done.8, bf16[2,4,128,128]{3,2,1,0:T(8,128)(2,1)S(1)} %copy-done.9), custom_call_target="tpu_custom_call" | custom-call | tf_op jit(solution)/shard_map/from_modes_4/pallas_call | solution.py:490
  89.0 1.0 copy-done.3
  90.0 0.8 copy-done.6
  90.8 17.9 %swap_6.1 = (bf16[16,2,64,256]{3,2,1,0:T(8,128)(2,1)}, bf16[64,256]{1,0:T(8,128)(2,1)}) custom-call(bf16[16,2,64,256]{3,2,1,0:T(8,128)(2,1)} %copy-done.3, bf16[16,64,256]{2,1,0:T(8,128)(2,1)} %copy-done.6), custom_call_target="tpu_custom_call" | custom-call | tf_op jit(solution)/shard_map/swap_6/pallas_call | solution.py:184
  110.6 33.0 %dense.1 = (bf16[16,16,64,256]{3,2,1,0:T(8,128)(2,1)}, bf16[16,16,64,256]{3,2,1,0:T(8,128)(2,1)}, f32[3,16,16,256]{3,2,1,0:T(8,128)}, f32[3,32,256]{2,1,0:T(8,12...) custom-call(bf16[32,64,256]{2,1,0:T(8,128)(2,1)} %bitcast.64, bf16[64,256]{1,0:T(8,128)(2,1)} %get-tuple-element.43.odd_ref, ...), custom_call_target="tpu_custom_call" | custom-call | tf_op jit(solution)/shard_map/dense/pallas_call | solution.py:623
  143.6 7.4 %halo.1 = (f32[3,2,16,256]{3,2,1,0:T(8,128)}, f32[3,2,16,256]{3,2,1,0:T(8,128)}, f32[3,32,256]{2,1,0:T(8,128)}, f32[3,32,256]{2,1,0:T(8,128)}, f32[4,8,256]{2,1,0:T(8,128)}) custom-call(f32[3,16,16,256]{3,2,1,0:T(8,128)} %get-tuple-element.47.field.field_ref, f32[3,32,256]{2,1,0:T(8,128)} %get-tuple-element.48.low, f32[3,32,256]{2,1,0:T(8,128)} %get-tuple-element.49.high, ...), custom_call_target="tpu_custom_call" | custom-call | tf_op jit(solution)/shard_map/halo/pallas_call | solution.py:830
  151.7 7.3 %stencil.1 = (f32[3,16,16,256]{3,2,1,0:T(8,128)}, f32[8,256]{1,0:T(8,128)}) custom-call(s32[2]{0:T(128)} %pad_add_fusion.place_ref, f32[3,16,16,256]{3,2,1,0:T(8,128)} %get-tuple-element.47.field.field_ref, f32[3,2,16,256]{3,2,1,0:T(8,128)} %get-tuple-element.51.y_low_ref, f32[3,2,16,256]{3,2,1,0:T(8,128)} %get-tuple-element.52.y_high_ref, ...), custom_call_target="tpu_custom_call" | custom-call | tf_op jit(solution)/shard_map/stencil/pallas_call | solution.py:934
  159.0 0.7 copy.48.out_w_ref
  159.6 20.3 %grad_dense.1 = (bf16[16,2,64,256]{3,2,1,0:T(8,128)(2,1)}, bf16[64,256]{1,0:T(8,128)(2,1)}, f32[128,128]{1,0:T(8,128)}) custom-call(bf16[16,16,64,256]{3,2,1,0:T(8,128)(2,1)} %get-tuple-element.45.hidden_ref, bf16[16,16,64,256]{3,2,1,0:T(8,128)(2,1)} %get-tuple-element.46.slope_ref, bf16[16,16,64,256]{3,2,1,0:T(8,128)(2,1)} %get-tuple-element.44.cells_ref, ...), custom_call_target="tpu_custom_call" | custom-call | tf_op jit(solution)/shard_map/grad_dense/pallas_call | solution.py:732
  180.0 29.5 %swap_7.1 = (bf16[16,2,64,256]{3,2,1,0:T(8,128)(2,1)}, bf16[16,64,256]{2,1,0:T(8,128)(2,1)}, f32[16,8,128]{2,1,0:T(8,128)}) custom-call(bf16[16,2,64,256]{3,2,1,0:T(8,128)(2,1)} %get-tuple-element.58.refs_0_, bf16[64,256]{1,0:T(8,128)(2,1)} %get-tuple-element.59.refs_1_, f32[16,8,128]{2,1,0:T(8,128)} %bitcast.69), custom_call_target="tpu_custom_call" | custom-call | tf_op jit(solution)/shard_map/swap_7/pallas_call | solution.py:184
  209.5 1.2 copy-done.2
  210.7 1.0 copy-done.5
  211.8 0.8 copy-done.10
  212.6 16.7 %to_modes_8.1 = (f32[16,8,256]{2,1,0:T(8,128)S(1)}, f32[16,8,128]{2,1,0:T(8,128)S(1)}) custom-call(bf16[16,2,64,256]{3,2,1,0:T(8,128)(2,1)S(1)} %copy-done.2, bf16[16,64,256]{2,1,0:T(8,128)(2,1)S(1)} %copy-done.5, bf16[256,1024]{1,0:T(8,128)(2,1)S(1)} %copy-done, bf16[2,4,128,128]{3,2,1,0:T(8,128)(2,1)S(1)} %copy-done.1, f32[16,8,128]{2,1,0:T(8,128)S(1)} %copy-done.10), custom_call_target="tpu_custom_call" | custom-call | tf_op jit(solution)/shard_map/to_modes_8/pallas_call | solution.py:459
  230.0 0.8 copy.53
  230.8 0.9 pad_maximum_fusion.1
  231.6 6.8 %weight_grad.1 = f32[8,32,64,128]{3,2,1,0:T(8,128)} custom-call(bf16[32,16,64]{2,1,0:T(8,128)(2,1)} %bitcast.66, bf16[32,16,128]{2,1,0:T(8,128)(2,1)} %bitcast.65, bf16[16,1024]{1,0:T(8,128)(2,1)} %constant.38.clone.mask_ref), custom_call_target="tpu_custom_call" | custom-call | tf_op jit(solution)/shard_map/weight_grad/pallas_call | solution.py:537
  (61 shorter events, 6.7 us)
Async XLA Ops:
  0.6 39.4 %copy-start = (bf16[256,1024]{1,0:T(8,128)(2,1)S(1)}, bf16[256,1024]{1,0:T(8,128)(2,1)}, u32[]{:S(2)}) copy-start(bf16[256,1024]{1,0:T(8,128)(2,1)} %constant.33.clone.refs_2_) | copy-start | bytes 1572868
  0.6 39.4 %copy-start.1 = (bf16[2,4,128,128]{3,2,1,0:T(8,128)(2,1)S(1)}, bf16[2,4,128,128]{3,2,1,0:T(8,128)(2,1)}, u32[]{:S(2)}) copy-start(bf16[2,4,128,128]{3,2,1,0:T(8,128)(2,1)} %constant.34.clone.refs_3_) | copy-start | bytes 786436
  15.9 49.0 %copy-start.8 = (bf16[1024,256]{1,0:T(8,128)(2,1)S(1)}, bf16[1024,256]{1,0:T(8,128)(2,1)}, u32[]{:S(2)}) copy-start(bf16[1024,256]{1,0:T(8,128)(2,1)} %constant.35.clone.y_table) | copy-start | bytes 1572868
  15.9 49.0 %copy-start.9 = (bf16[2,4,128,128]{3,2,1,0:T(8,128)(2,1)S(1)}, bf16[2,4,128,128]{3,2,1,0:T(8,128)(2,1)}, u32[]{:S(2)}) copy-start(bf16[2,4,128,128]{3,2,1,0:T(8,128)(2,1)} %constant.36.clone.z_table) | copy-start | bytes 786436
  15.9 92.8 %copy-start.11 = (bf16[64,64]{1,0:T(8,128)(2,1)S(1)}, bf16[64,64]{1,0:T(8,128)(2,1)}, u32[]{:S(2)}) copy-start(bf16[64,64]{1,0:T(8,128)(2,1)} %param.18) | copy-start | bytes 24580
  15.9 93.5 %copy-start.12 = (bf16[64,3]{0,1:T(4,128)(2,1)S(1)}, bf16[64,3]{0,1:T(4,128)(2,1)}, u32[]{:S(2)}) copy-start(bf16[64,3]{0,1:T(4,128)(2,1)} %param.20) | copy-start | bytes 1156
  15.9 94.1 %copy-start.13 = (f32[64]{0:T(128)S(1)}, f32[64]{0:T(128)}, u32[]{:S(2)}) copy-start(f32[64]{0:T(128)} %param.19) | copy-start | bytes 772
  40.1 1.2 copy-start.4
  41.3 1.0 copy-start.7
  89.0 1.0 copy-start.3
  90.0 0.8 copy-start.6
  209.5 1.2 copy-start.2
  210.7 1.0 copy-start.5
  211.8 0.8 copy-start.10

commit v3 on v2

--- a/solution.py
+++ b/solution.py
@@ -22,6 +22,8 @@
 DENSITY = 1.0 / math.sqrt(math.pi)
 MESH = pl.DeviceIdType.MESH
 ANY = pl.BlockSpec(memory_space=pl.ANY)
+NEAR = pl.BlockSpec(memory_space=pltpu.VMEM)
+FAR = pl.BlockSpec(memory_space=pltpu.HBM)
 
 
 def np_table(length):
@@ -40,7 +42,7 @@
     forward[16] = cos_x[:, 16]
     forward[17:32] = sin_x[:, 1:16].T
     forward[32] = sin_x[:, 16]
-    inverse = np.zeros((64, NX))
+    inverse = np.zeros((40, NX))
     inverse[33:36] = 1.0
     inverse[0:32:2] = forward[:16]
     inverse[1:32:2] = forward[16:32]
@@ -169,7 +171,7 @@
         finish()
 
 
-def swap(axis, count, collective_id, *operands):
+def swap(axis, count, collective_id, spaces, *operands):
     modes = tuple(mode for mode, _ in operands)
     args = [value for _, value in operands]
     outs = []
@@ -184,12 +186,12 @@
     result = pl.pallas_call(
         functools.partial(swap_kernel, axis, count, modes),
         out_shape=outs,
-        in_specs=[ANY] * size,
-        out_specs=[ANY] * size,
+        in_specs=[spaces[0]] * size,
+        out_specs=[spaces[1]] * size,
         scratch_shapes=[pltpu.SemaphoreType.DMA((count,))] * (2 * size)
         + [pltpu.SemaphoreType.DMA((size,))],
         compiler_params=pltpu.CompilerParams(
-            collective_id=collective_id, has_side_effects=True
+            collective_id=collective_id, has_side_effects=True, vmem_limit_bytes=16 << 20
         ),
         name=f"swap_{collective_id}",
     )(*args)
@@ -569,24 +571,18 @@
                 start = 2112 + part * 64
                 rows[half, start : start + 64, :] = jnp.broadcast_to(piece, (64, 128))
                 rest = rest - piece
-            rows[half, 2304:3072, :] = jnp.zeros((768, 128), F32)
+            rows[half, 2304:2560, :] = jnp.zeros((256, 128), F32)
 
     def plane(k, carry):
         y = step * YB + k
         for q in range(QZ):
             picked = jnp.concatenate(
-                [rows[half, pl.ds(y * QZ + q, 48, stride=64), :] for half in range(2)], axis=1
-            )
-            picked = jnp.concatenate(
-                [jnp.zeros((64, NX), F32), picked, jnp.zeros((16, NX), F32)], axis=0
-            )
-            left = picked.T.astype(BF16)
+                [rows[half, pl.ds(y * QZ + q, 40, stride=64), :] for half in range(2)], axis=1
+            ).astype(BF16)
+            spectral = dot(picked, table_ref[...], TN)
             for inner in range(4):
                 z = q * 4 + inner
-                pre = dot(
-                    left[inner * C : inner * C + C] + point_ref[...],
-                    jnp.concatenate([cells_ref[k, z], table_ref[...]], axis=0),
-                )
+                pre = spectral[inner * C : inner * C + C] + dot(point_ref[...], cells_ref[k, z])
                 scaled = pre * math.sqrt(0.5)
                 normal_cdf = 0.5 * lax.erf(scaled) + 0.5
                 decay = jnp.exp2(scaled * scaled * -math.log2(math.e))
@@ -627,8 +623,8 @@
             whole((GY * 2, 64, NX)),
             whole((64, NX)),
             cell_spec,
-            whole((64, NX)),
-            whole((C, 128)),
+            whole((40, NX)),
+            whole((C, C)),
             whole((1, 128)),
             whole((8, C)),
             pl.BlockSpec(memory_space=pltpu.SMEM),
@@ -649,7 +645,7 @@
             jax.ShapeDtypeStruct((3, 32, NX), F32),
             jax.ShapeDtypeStruct((4, 8, NX), F32),
         ],
-        scratch_shapes=[pltpu.VMEM((2, 48 * 64, 128), F32)],
+        scratch_shapes=[pltpu.VMEM((2, 40 * 64, 128), F32)],
         compiler_params=params(),
         name="dense",
     )(
@@ -657,7 +653,7 @@
         odd,
         cells,
         const(tables()[1]),
-        jnp.pad(point_weight.T, ((0, 0), (0, C))),
+        point_weight.T,
         jnp.concatenate([point_bias, point_bias])[None],
         out_w,
         out_bias,
@@ -952,7 +948,7 @@
 def on_device(field_in, spectral_weight, point_weight, point_bias, out_weight, out_bias):
     place = jnp.stack([lax.axis_index("gy"), lax.axis_index("gz")]).astype(jnp.int32)
     cells, rows, odd = x_transform(field_in)
-    rows, odd = swap("gy", GY, 1, ("swap", rows), ("to0", odd))
+    rows, odd = swap("gy", GY, 1, (FAR, NEAR), ("swap", rows), ("to0", odd))
     modes_in = to_kx(to_modes(2, SCALE, rows, odd).astype(BF16))
 
     mixed = jnp.einsum(
@@ -963,7 +959,7 @@
     modes_out = jnp.stack([real, imag], axis=3)
 
     rows, odd = from_modes(4, from_kx(modes_out))
-    rows, odd = swap("gy", GY, 6, ("swap", rows), ("from0", odd))
+    rows, odd = swap("gy", GY, 6, (NEAR, FAR), ("swap", rows), ("from0", odd))
 
     hidden, slope, field_b, *edges = dense(
         rows, odd, cells, point_weight, point_bias, out_weight, out_bias
@@ -971,7 +967,7 @@
     grad_b, loss_rows = stencil(place, field_b, *halo(10, field_b, *edges))
     rows, odd, small = grad_dense(hidden, slope, cells, grad_b, out_weight, loss_rows)
     small = small.reshape(GY, 8, 128)
-    rows, odd, small = swap("gy", GY, 7, ("swap", rows), ("to0", odd), ("swap", small))
+    rows, odd, small = swap("gy", GY, 7, (FAR, NEAR), ("swap", rows), ("to0", odd), ("swap", small))
     dealt, small = to_modes(8, 1.0, rows, odd, small)
     small = small.reshape(128, 128)
     grad_modes = to_kx(dealt.astype(BF16))

time: 243 us -> 240 us (0.988)
  no operation moved by 1% of the time
where the time goes in v3:
time: 240 us; the launch traced here: 239 us
  Pallas kernels  218 us (91%)
  local copies, waits for them, and re-layouts  12.5 us (5%)
  other arithmetic  3.49 us (1%)
  matrix products  3.37 us (1%)
    pallas_call x3, Pallas kernels, swap(): pl.pallas_call(functools.partial(swap_kernel, axis, count, modes), out_sh...  71.5 us
    pallas_call x2, Pallas kernels, to_modes(): pl.pallas_call(functools.partial(to_modes_kernel, factor, small is not No...  34.4 us
    pallas_call x1, Pallas kernels, dense(): pl.pallas_call(dense_kernel, grid=(LY // YB,), in_specs=[whole((GY * 2, 6...  31 us
    pallas_call x1, Pallas kernels, from_modes(): pl.pallas_call(from_modes_kernel, out_shape=[jax.ShapeDtypeStruct((GY, 2,...  24.1 us
    pallas_call x1, Pallas kernels, grad_dense(): pl.pallas_call(grad_kernel, grid=(LY // YB,), in_specs=[cell_spec, cell_s...  20.3 us
    pallas_call x1, Pallas kernels, x_transform(): pl.pallas_call(x_kernel, grid=(LY // YB,), in_specs=[pl.BlockSpec((C, YB,...  15.3 us
    pallas_call x1, Pallas kernels, stencil(): pl.pallas_call(stencil_kernel, in_specs=[pl.BlockSpec(memory_space=pltpu....  7.25 us
    unnamed x31, local copies, waits for them, and re-layouts  7.18 us

profile of v3, /device:TPU:1, one launch (start us, length us, event | category | flops | bytes accessed | tf_op | source)
XLA Modules:
  0.0 239.1 jit_solution(16434315639566332429)
XLA Ops:
  0.7 15.3 %x_transform.1 = (bf16[16,16,64,256]{3,2,1,0:T(8,128)(2,1)}, bf16[16,2,64,256]{3,2,1,0:T(8,128)(2,1)}, bf16[64,256]{1,0:T(8,128)(2,1)}) custom-call(bf16[64,16,16,256]{3,2,1,0:T(8,128)(2,1)} %field_ref.1, bf16[40,256]{1,0:T(8,128)(2,1)} %constant.32.clone.table_ref), custom_call_target="tpu_custom_call" | custom-call | tf_op jit(solution)/shard_map/x_transform/pallas_call | solution.py:239
  16.0 1.2 copy-done.4
  17.2 0.8 copy-done.10
  18.0 23.7 %swap_1.1 = (bf16[16,2,64,256]{3,2,1,0:T(8,128)(2,1)S(1)}, bf16[16,64,256]{2,1,0:T(8,128)(2,1)S(1)}) custom-call(bf16[16,2,64,256]{3,2,1,0:T(8,128)(2,1)S(1)} %copy-done.4, bf16[64,256]{1,0:T(8,128)(2,1)S(1)} %copy-done.10), custom_call_target="tpu_custom_call" | custom-call | tf_op jit(solution)/shard_map/swap_1/pallas_call | solution.py:186
  41.7 17.5 %to_modes_2.1 = f32[16,8,256]{2,1,0:T(8,128)S(1)} custom-call(bf16[16,2,64,256]{3,2,1,0:T(8,128)(2,1)S(1)} %get-tuple-element.38.refs_0_, bf16[16,64,256]{2,1,0:T(8,128)(2,1)S(1)} %get-tuple-element.39.refs_1_, bf16[256,1024]{1,0:T(8,128)(2,1)S(1)} %copy-done, bf16[2,4,128,128]{3,2,1,0:T(8,128)(2,1)S(1)} %copy-done.2), custom_call_target="tpu_custom_call" | custom-call | tf_op jit(solution)/shard_map/to_modes_2/pallas_call | solution.py:461
  59.5 3.4 %fusion = f32[4,2,32,2,128]{4,3,2,1,0:T(2,128)S(1)} fusion(bf16[4,2,32,64,128]{4,3,2,1,0:T(8,128)(2,1)} %param.17, bf16[15,4,2,2,64]{4,3,0,2,1:T(2,128)(2,1)S(1)} %rev.9, bf16[1,4,2,2,64]{4,3,0,2,1:T(2,128)(2,1)S(1)} %slice_bitcast_fusion.4, bf16[16,4,2,2,64]{4,3,0,2,1:T(2,128)(2,1)S(1)} %copy_bitcast_fusion.2), kind=kOutput, calls=%fused_computation.9 | convolution fusion | flops 8585216 | bytes 4521984 | tf_op jit(solution)/shard_map/abkpi,abkio->abkpo/dot_general | solution.py:954
  62.9 0.6 slice_subtract_fusion
  64.5 24.1 %from_modes_4.1 = (bf16[16,2,64,256]{3,2,1,0:T(8,128)(2,1)S(1)}, bf16[16,64,256]{2,1,0:T(8,128)(2,1)S(1)}) custom-call(f32[16,8,256]{2,1,0:T(8,128)S(1)} %reshape.46.modes, bf16[1024,256]{1,0:T(8,128)(2,1)S(1)} %copy-done.5, bf16[2,4,128,128]{3,2,1,0:T(8,128)(2,1)S(1)} %copy-done.6), custom_call_target="tpu_custom_call" | custom-call | tf_op jit(solution)/shard_map/from_modes_4/pallas_call | solution.py:492
  88.6 18.3 %swap_6.1 = (bf16[16,2,64,256]{3,2,1,0:T(8,128)(2,1)S(1)}, bf16[64,256]{1,0:T(8,128)(2,1)S(1)}) custom-call(bf16[16,2,64,256]{3,2,1,0:T(8,128)(2,1)S(1)} %get-tuple-element.40.refs_0_, bf16[16,64,256]{2,1,0:T(8,128)(2,1)S(1)} %get-tuple-element.41.refs_1_), custom_call_target="tpu_custom_call" | custom-call | tf_op jit(solution)/shard_map/swap_6/pallas_call | solution.py:186
  107.0 1.0 copy-done.1
  108.6 0.7 copy.47
  110.4 31.0 %dense.1 = (bf16[16,16,64,256]{3,2,1,0:T(8,128)(2,1)}, bf16[16,16,64,256]{3,2,1,0:T(8,128)(2,1)}, f32[3,16,16,256]{3,2,1,0:T(8,128)}, f32[3,32,256]{2,1,0:T(8,12...) custom-call(bf16[32,64,256]{2,1,0:T(8,128)(2,1)} %bitcast.59, bf16[64,256]{1,0:T(8,128)(2,1)} %copy-done.8, ...), custom_call_target="tpu_custom_call" | custom-call | tf_op jit(solution)/shard_map/dense/pallas_call | solution.py:619
  141.5 7.0 %halo.1 = (f32[3,2,16,256]{3,2,1,0:T(8,128)}, f32[3,2,16,256]{3,2,1,0:T(8,128)}, f32[3,32,256]{2,1,0:T(8,128)}, f32[3,32,256]{2,1,0:T(8,128)}, f32[4,8,256]{2,1,0:T(8,128)}) custom-call(f32[3,16,16,256]{3,2,1,0:T(8,128)} %get-tuple-element.47.field.field_ref, f32[3,32,256]{2,1,0:T(8,128)} %get-tuple-element.48.low, f32[3,32,256]{2,1,0:T(8,128)} %get-tuple-element.49.high, ...), custom_call_target="tpu_custom_call" | custom-call | tf_op jit(solution)/shard_map/halo/pallas_call | solution.py:826
  149.0 7.3 %stencil.1 = (f32[3,16,16,256]{3,2,1,0:T(8,128)}, f32[8,256]{1,0:T(8,128)}) custom-call(s32[2]{0:T(128)} %pad_add_fusion.place_ref, f32[3,16,16,256]{3,2,1,0:T(8,128)} %get-tuple-element.47.field.field_ref, f32[3,2,16,256]{3,2,1,0:T(8,128)} %get-tuple-element.51.y_low_ref, f32[3,2,16,256]{3,2,1,0:T(8,128)} %get-tuple-element.52.y_high_ref, ...), custom_call_target="tpu_custom_call" | custom-call | tf_op jit(solution)/shard_map/stencil/pallas_call | solution.py:930
  156.3 0.7 copy.48.out_w_ref
  157.0 20.3 %grad_dense.1 = (bf16[16,2,64,256]{3,2,1,0:T(8,128)(2,1)}, bf16[64,256]{1,0:T(8,128)(2,1)}, f32[128,128]{1,0:T(8,128)}) custom-call(bf16[16,16,64,256]{3,2,1,0:T(8,128)(2,1)} %get-tuple-element.45.hidden_ref, bf16[16,16,64,256]{3,2,1,0:T(8,128)(2,1)} %get-tuple-element.46.slope_ref, bf16[16,16,64,256]{3,2,1,0:T(8,128)(2,1)} %get-tuple-element.44.cells_ref, ...), custom_call_target="tpu_custom_call" | custom-call | tf_op jit(solution)/shard_map/grad_dense/pallas_call | solution.py:728
  177.3 1.2 copy-done.3
  178.6 0.8 copy-done.7
  179.4 0.8 copy-done.9
  180.2 29.5 %swap_7.1 = (bf16[16,2,64,256]{3,2,1,0:T(8,128)(2,1)S(1)}, bf16[16,64,256]{2,1,0:T(8,128)(2,1)S(1)}, f32[16,8,128]{2,1,0:T(8,128)S(1)}) custom-call(bf16[16,2,64,256]{3,2,1,0:T(8,128)(2,1)S(1)} %copy-done.3, bf16[64,256]{1,0:T(8,128)(2,1)S(1)} %copy-done.9, f32[16,8,128]{2,1,0:T(8,128)S(1)} %bitcast.60), custom_call_target="tpu_custom_call" | custom-call | tf_op jit(solution)/shard_map/swap_7/pallas_call | solution.py:186
  209.6 16.9 %to_modes_8.1 = (f32[16,8,256]{2,1,0:T(8,128)S(1)}, f32[16,8,128]{2,1,0:T(8,128)S(1)}) custom-call(bf16[16,2,64,256]{3,2,1,0:T(8,128)(2,1)S(1)} %get-tuple-element.61.refs_0_, bf16[16,64,256]{2,1,0:T(8,128)(2,1)S(1)} %get-tuple-element.62.refs_1_, bf16[256,1024]{1,0:T(8,128)(2,1)S(1)} %copy-done, bf16[2,4,128,128]{3,2,1,0:T(8,128)(2,1)S(1)} %copy-done.2, ...), custom_call_target="tpu_custom_call" | custom-call | tf_op jit(solution)/shard_map/to_modes_8/pallas_call | solution.py:461
  227.2 0.8 copy.53
  227.9 0.9 pad_maximum_fusion.1
  228.8 6.8 %weight_grad.1 = f32[8,32,64,128]{3,2,1,0:T(8,128)} custom-call(bf16[32,16,64]{2,1,0:T(8,128)(2,1)} %bitcast.67, bf16[32,16,128]{2,1,0:T(8,128)(2,1)} %bitcast.66, bf16[16,1024]{1,0:T(8,128)(2,1)} %constant.38.clone.mask_ref), custom_call_target="tpu_custom_call" | custom-call | tf_op jit(solution)/shard_map/weight_grad/pallas_call | solution.py:539
  (60 shorter events, 6.6 us)
Async XLA Ops:
  0.6 41.1 %copy-start = (bf16[256,1024]{1,0:T(8,128)(2,1)S(1)}, bf16[256,1024]{1,0:T(8,128)(2,1)}, u32[]{:S(2)}) copy-start(bf16[256,1024]{1,0:T(8,128)(2,1)} %constant.33.clone.refs_2_) | copy-start | bytes 1572868
  0.6 41.0 %copy-start.2 = (bf16[2,4,128,128]{3,2,1,0:T(8,128)(2,1)S(1)}, bf16[2,4,128,128]{3,2,1,0:T(8,128)(2,1)}, u32[]{:S(2)}) copy-start(bf16[2,4,128,128]{3,2,1,0:T(8,128)(2,1)} %constant.34.clone.refs_3_) | copy-start | bytes 786436
  0.7 63.9 %copy-start.5 = (bf16[1024,256]{1,0:T(8,128)(2,1)S(1)}, bf16[1024,256]{1,0:T(8,128)(2,1)}, u32[]{:S(2)}) copy-start(bf16[1024,256]{1,0:T(8,128)(2,1)} %constant.35.clone.y_table) | copy-start | bytes 1572868
  0.7 63.9 %copy-start.6 = (bf16[2,4,128,128]{3,2,1,0:T(8,128)(2,1)S(1)}, bf16[2,4,128,128]{3,2,1,0:T(8,128)(2,1)}, u32[]{:S(2)}) copy-start(bf16[2,4,128,128]{3,2,1,0:T(8,128)(2,1)} %constant.36.clone.z_table) | copy-start | bytes 786436
  0.7 107.9 %copy-start.11 = (bf16[64,64]{1,0:T(8,128)(2,1)S(1)}, bf16[64,64]{1,0:T(8,128)(2,1)}, u32[]{:S(2)}) copy-start(bf16[64,64]{1,0:T(8,128)(2,1)} %param.18) | copy-start | bytes 24580
  16.0 93.3 %copy-start.12 = (bf16[64,3]{0,1:T(4,128)(2,1)S(1)}, bf16[64,3]{0,1:T(4,128)(2,1)}, u32[]{:S(2)}) copy-start(bf16[64,3]{0,1:T(4,128)(2,1)} %param.20) | copy-start | bytes 1156
  16.0 93.9 %copy-start.13 = (f32[64]{0:T(128)S(1)}, f32[64]{0:T(128)}, u32[]{:S(2)}) copy-start(f32[64]{0:T(128)} %param.19) | copy-start | bytes 772
  16.0 1.2 copy-start.4
  17.2 0.8 copy-start.10
  107.0 1.0 copy-start.1
  108.0 0.6 copy-start.8
  177.3 1.2 copy-start.3
  178.6 0.8 copy-start.7
  179.4 0.8 copy-start.9

commit v4 on v3

--- a/solution.py
+++ b/solution.py
@@ -80,7 +80,7 @@
     return pl.BlockSpec(shape, lambda *_: (0,) * len(shape))
 
 
-def params(limit=56 << 20):
+def params(limit=50 << 20):
     return pltpu.CompilerParams(vmem_limit_bytes=limit)
 
 

time: 240 us -> 234 us (0.975)
  Pallas kernels: 218 us -> 213 us
    unnamed x31 -> x47, local copies, waits for them, and re-layouts: 7.18 us -> 9.22 us
where the time goes in v4:
time: 234 us; the launch traced here: 233 us
  Pallas kernels  213 us (91%)
  local copies, waits for them, and re-layouts  12.8 us (5%)
  matrix products  3.37 us (1%)
    pallas_call x3, Pallas kernels, swap(): pl.pallas_call(functools.partial(swap_kernel, axis, count, modes), out_sh...  71.8 us
    pallas_call x2, Pallas kernels, to_modes(): pl.pallas_call(functools.partial(to_modes_kernel, factor, small is not No...  34.3 us
    pallas_call x1, Pallas kernels, dense(): pl.pallas_call(dense_kernel, grid=(LY // YB,), in_specs=[whole((GY * 2, 6...  30.5 us
    pallas_call x1, Pallas kernels, from_modes(): pl.pallas_call(from_modes_kernel, out_shape=[jax.ShapeDtypeStruct((GY, 2,...  24.1 us
    pallas_call x1, Pallas kernels, grad_dense(): pl.pallas_call(grad_kernel, grid=(LY // YB,), in_specs=[cell_spec, cell_s...  19.3 us
    pallas_call x1, Pallas kernels, x_transform(): pl.pallas_call(x_kernel, grid=(LY // YB,), in_specs=[pl.BlockSpec((C, YB,...  14.8 us
    unnamed x47, local copies, waits for them, and re-layouts  9.22 us
    pallas_call x1, Pallas kernels, halo(): pl.pallas_call(halo_kernel, out_shape=[side, side, edge, edge, jax.ShapeD...  6.85 us

profile of v4, /device:TPU:1, one launch (start us, length us, event | category | flops | bytes accessed | tf_op | source)
XLA Modules:
  0.0 233.2 jit_solution(2764492939612867735)
XLA Ops:
  0.7 0.8 copy-done.12
  1.5 14.8 %x_transform.1 = (bf16[16,16,64,256]{3,2,1,0:T(8,128)(2,1)}, bf16[16,2,64,256]{3,2,1,0:T(8,128)(2,1)S(1)}, bf16[64,256]{1,0:T(8,128)(2,1)S(1)}) custom-call(bf16[64,16,16,256]{3,2,1,0:T(8,128)(2,1)} %field_ref.1, bf16[40,256]{1,0:T(8,128)(2,1)S(1)} %copy-done.12), custom_call_target="tpu_custom_call" | custom-call | tf_op jit(solution)/shard_map/x_transform/pallas_call | solution.py:239
  16.3 23.8 %swap_1.1 = (bf16[16,2,64,256]{3,2,1,0:T(8,128)(2,1)S(1)}, bf16[16,64,256]{2,1,0:T(8,128)(2,1)S(1)}) custom-call(bf16[16,2,64,256]{3,2,1,0:T(8,128)(2,1)S(1)} %get-tuple-element.36.refs_0_, bf16[64,256]{1,0:T(8,128)(2,1)S(1)} %get-tuple-element.37.refs_1_), custom_call_target="tpu_custom_call" | custom-call | tf_op jit(solution)/shard_map/swap_1/pallas_call | solution.py:186
  40.2 17.5 %to_modes_2.1 = f32[16,8,256]{2,1,0:T(8,128)S(1)} custom-call(bf16[16,2,64,256]{3,2,1,0:T(8,128)(2,1)S(1)} %get-tuple-element.38.refs_0_, bf16[16,64,256]{2,1,0:T(8,128)(2,1)S(1)} %get-tuple-element.39.refs_1_, bf16[256,1024]{1,0:T(8,128)(2,1)S(1)} %copy-done.2, bf16[2,4,128,128]{3,2,1,0:T(8,128)(2,1)S(1)} %copy-done.3), custom_call_target="tpu_custom_call" | custom-call | tf_op jit(solution)/shard_map/to_modes_2/pallas_call | solution.py:461
  58.0 3.4 %fusion = f32[4,2,32,2,128]{4,3,2,1,0:T(2,128)S(1)} fusion(bf16[4,2,32,64,128]{4,3,2,1,0:T(8,128)(2,1)} %param.17, bf16[15,4,2,2,64]{4,3,0,2,1:T(2,128)(2,1)S(1)} %rev.9, bf16[1,4,2,2,64]{4,3,0,2,1:T(2,128)(2,1)S(1)} %slice_bitcast_fusion.4, bf16[16,4,2,2,64]{4,3,0,2,1:T(2,128)(2,1)S(1)} %copy_bitcast_fusion.2), kind=kOutput, calls=%fused_computation.9 | convolution fusion | flops 8585216 | bytes 4521984 | tf_op jit(solution)/shard_map/abkpi,abkio->abkpo/dot_general | solution.py:954
  61.4 0.6 slice_subtract_fusion
  63.0 24.1 %from_modes_4.1 = (bf16[16,2,64,256]{3,2,1,0:T(8,128)(2,1)S(1)}, bf16[16,64,256]{2,1,0:T(8,128)(2,1)S(1)}) custom-call(f32[16,8,256]{2,1,0:T(8,128)S(1)} %reshape.46.modes, bf16[1024,256]{1,0:T(8,128)(2,1)S(1)} %copy-done.4, bf16[2,4,128,128]{3,2,1,0:T(8,128)(2,1)S(1)} %copy-done.5), custom_call_target="tpu_custom_call" | custom-call | tf_op jit(solution)/shard_map/from_modes_4/pallas_call | solution.py:492
  87.1 18.3 %swap_6.1 = (bf16[16,2,64,256]{3,2,1,0:T(8,128)(2,1)S(1)}, bf16[64,256]{1,0:T(8,128)(2,1)S(1)}) custom-call(bf16[16,2,64,256]{3,2,1,0:T(8,128)(2,1)S(1)} %get-tuple-element.40.refs_0_, bf16[16,64,256]{2,1,0:T(8,128)(2,1)S(1)} %get-tuple-element.41.refs_1_), custom_call_target="tpu_custom_call" | custom-call | tf_op jit(solution)/shard_map/swap_6/pallas_call | solution.py:186
  105.6 30.5 %dense.1 = (bf16[16,16,64,256]{3,2,1,0:T(8,128)(2,1)}, bf16[16,16,64,256]{3,2,1,0:T(8,128)(2,1)}, f32[3,16,16,256]{3,2,1,0:T(8,128)S(1)}, f32[3,32,256]{2,1,0:T(...) custom-call(bf16[32,64,256]{2,1,0:T(8,128)(2,1)S(1)} %bitcast.59, ...), custom_call_target="tpu_custom_call" | custom-call | tf_op jit(solution)/shard_map/dense/pallas_call | solution.py:619
  136.2 0.9 copy-done
  137.1 0.6 copy-done.10
  137.7 0.6 copy-done.11
  138.9 6.9 %halo.1 = (f32[3,2,16,256]{3,2,1,0:T(8,128)}, f32[3,2,16,256]{3,2,1,0:T(8,128)}, f32[3,32,256]{2,1,0:T(8,128)}, f32[3,32,256]{2,1,0:T(8,128)}, f32[4,8,256]{2,1,0:T(8,128)}) custom-call(f32[3,16,16,256]{3,2,1,0:T(8,128)} %copy-done, f32[3,32,256]{2,1,0:T(8,128)} %copy-done.10, f32[3,32,256]{2,1,0:T(8,128)} %copy-done.11, f32[4,8,256]{2,1,0:T(8,128)} %copy-done.16), custom_call_target="tpu_custom_call" | custom-call | tf_op jit(solution)/shard_map/halo/pallas_call | solution.py:826
  145.9 1.1 copy-done.1
  147.0 0.9 copy-done.6
  147.9 0.9 copy-done.7
  148.8 0.9 copy-done.8
  149.7 0.9 copy-done.9
  150.6 0.8 copy-done.15
  151.3 5.7 %stencil.1 = (f32[3,16,16,256]{3,2,1,0:T(8,128)S(1)}, f32[8,256]{1,0:T(8,128)S(1)}) custom-call(s32[2]{0:T(128)S(1)} %pad_add_fusion.place_ref, f32[3,16,16,256]{3,2,1,0:T(8,128)S(1)} %copy-done.1, f32[3,2,16,256]{3,2,1,0:T(8,128)S(1)} %copy-done.6, f32[3,2,16,256]{3,2,1,0:T(8,128)S(1)} %copy-done.7, f32[3,32,256]{2,1,0:T(8,128)S(1)} %copy-done.8, ...), custom_call_target="tpu_custom_call" | custom-call | tf_op jit(solution)/shard_map/stencil/pallas_call | solution.py:930
  157.2 19.3 %grad_dense.1 = (bf16[16,2,64,256]{3,2,1,0:T(8,128)(2,1)S(1)}, bf16[64,256]{1,0:T(8,128)(2,1)S(1)}, f32[128,128]{1,0:T(8,128)S(1)}) custom-call(bf16[16,16,64,256]{3,2,1,0:T(8,128)(2,1)} %get-tuple-element.45.hidden_ref, bf16[16,16,64,256]{3,2,1,0:T(8,128)(2,1)} %get-tuple-element.46.slope_ref, bf16[16,16,64,256]{3,2,1,0:T(8,128)(2,1)} %get-tuple-element.44.cells_ref, ...), custom_call_target="tpu_custom_call" | custom-call | tf_op jit(solution)/shard_map/grad_dense/pallas_call | solution.py:728
  176.5 29.7 %swap_7.1 = (bf16[16,2,64,256]{3,2,1,0:T(8,128)(2,1)S(1)}, bf16[16,64,256]{2,1,0:T(8,128)(2,1)S(1)}, f32[16,8,128]{2,1,0:T(8,128)S(1)}) custom-call(bf16[16,2,64,256]{3,2,1,0:T(8,128)(2,1)S(1)} %get-tuple-element.58.refs_0_, bf16[64,256]{1,0:T(8,128)(2,1)S(1)} %get-tuple-element.59.refs_1_, f32[16,8,128]{2,1,0:T(8,128)S(1)} %bitcast.63), custom_call_target="tpu_custom_call" | custom-call | tf_op jit(solution)/shard_map/swap_7/pallas_call | solution.py:186
  206.2 16.9 %to_modes_8.1 = (f32[16,8,256]{2,1,0:T(8,128)S(1)}, f32[16,8,128]{2,1,0:T(8,128)S(1)}) custom-call(bf16[16,2,64,256]{3,2,1,0:T(8,128)(2,1)S(1)} %get-tuple-element.61.refs_0_, bf16[16,64,256]{2,1,0:T(8,128)(2,1)S(1)} %get-tuple-element.62.refs_1_, bf16[256,1024]{1,0:T(8,128)(2,1)S(1)} %copy-done.2, bf16[2,4,128,128]{3,2,1,0:T(8,128)(2,1)S(1)} %copy-done.3, ...), custom_call_target="tpu_custom_call" | custom-call | tf_op jit(solution)/shard_map/to_modes_8/pallas_call | solution.py:461
  224.1 5.5 %weight_grad.1 = f32[8,32,64,128]{3,2,1,0:T(8,128)} custom-call(bf16[32,16,64]{2,1,0:T(8,128)(2,1)S(1)} %bitcast.61, bf16[32,16,128]{2,1,0:T(8,128)(2,1)S(1)} %bitcast.60, bf16[16,1024]{1,0:T(8,128)(2,1)S(1)} %copy-done.14), custom_call_target="tpu_custom_call" | custom-call | tf_op jit(solution)/shard_map/weight_grad/pallas_call | solution.py:539
  (76 shorter events, 5.6 us)
Async XLA Ops:
  0.6 39.6 %copy-start.2 = (bf16[256,1024]{1,0:T(8,128)(2,1)S(1)}, bf16[256,1024]{1,0:T(8,128)(2,1)}, u32[]{:S(2)}) copy-start(bf16[256,1024]{1,0:T(8,128)(2,1)} %constant.33.clone.refs_2_) | copy-start | bytes 1572868
  0.6 39.5 %copy-start.3 = (bf16[2,4,128,128]{3,2,1,0:T(8,128)(2,1)S(1)}, bf16[2,4,128,128]{3,2,1,0:T(8,128)(2,1)}, u32[]{:S(2)}) copy-start(bf16[2,4,128,128]{3,2,1,0:T(8,128)(2,1)} %constant.34.clone.refs_3_) | copy-start | bytes 786436
  0.7 0.8 copy-start.12
  16.3 46.8 %copy-start.4 = (bf16[1024,256]{1,0:T(8,128)(2,1)S(1)}, bf16[1024,256]{1,0:T(8,128)(2,1)}, u32[]{:S(2)}) copy-start(bf16[1024,256]{1,0:T(8,128)(2,1)} %constant.35.clone.y_table) | copy-start | bytes 1572868
  16.3 46.8 %copy-start.5 = (bf16[2,4,128,128]{3,2,1,0:T(8,128)(2,1)S(1)}, bf16[2,4,128,128]{3,2,1,0:T(8,128)(2,1)}, u32[]{:S(2)}) copy-start(bf16[2,4,128,128]{3,2,1,0:T(8,128)(2,1)} %constant.36.clone.z_table) | copy-start | bytes 786436
  16.3 89.1 %copy-start.19 = (bf16[64,64]{1,0:T(8,128)(2,1)S(1)}, bf16[64,64]{1,0:T(8,128)(2,1)}, u32[]{:S(2)}) copy-start(bf16[64,64]{1,0:T(8,128)(2,1)} %param.18) | copy-start | bytes 24580
  16.3 89.2 %copy-start.20 = (bf16[64,3]{0,1:T(4,128)(2,1)S(1)}, bf16[64,3]{0,1:T(4,128)(2,1)}, u32[]{:S(2)}) copy-start(bf16[64,3]{0,1:T(4,128)(2,1)} %param.20) | copy-start | bytes 1156
  16.3 89.3 %copy-start.21 = (f32[64]{0:T(128)S(1)}, f32[64]{0:T(128)}, u32[]{:S(2)}) copy-start(f32[64]{0:T(128)} %param.19) | copy-start | bytes 772
  16.3 89.3 %copy-start.17 = (bf16[40,256]{1,0:T(8,128)(2,1)S(1)}, bf16[40,256]{1,0:T(8,128)(2,1)}, u32[]{:S(2)}) copy-start(bf16[40,256]{1,0:T(8,128)(2,1)} %constant.37.clone.table_ref) | copy-start | bytes 61444
  16.3 89.3 %copy-start.18 = (f32[3]{0:T(128)S(1)}, f32[3]{0:T(128)}, u32[]{:S(2)}) copy-start(f32[3]{0:T(128)} %out_b_ref.1) | copy-start | bytes 40
  62.3 94.9 %copy-start.13 = (bf16[40,256]{1,0:T(8,128)(2,1)S(1)}, bf16[40,256]{1,0:T(8,128)(2,1)}, u32[]{:S(2)}) copy-start(bf16[40,256]{1,0:T(8,128)(2,1)} %constant.32.clone.table_ref) | copy-start | bytes 61444
  136.2 0.9 copy-start
  137.1 0.6 copy-start.10
  137.7 0.6 copy-start.11
  138.3 0.6 copy-start.16
  145.9 1.1 copy-start.1
  147.0 0.9 copy-start.6
  147.9 0.9 copy-start.7
  148.8 0.9 copy-start.8
  149.7 0.9 copy-start.9
  150.6 0.8 copy-start.15
  157.2 66.9 %copy-start.14 = (bf16[16,1024]{1,0:T(8,128)(2,1)S(1)}, bf16[16,1024]{1,0:T(8,128)(2,1)}, u32[]{:S(2)}) copy-start(bf16[16,1024]{1,0:T(8,128)(2,1)} %constant.38.clone.mask_ref) | copy-start | bytes 98308
